TPU v7x, 256 devices: a whole 4x4x8 slice. The times are simulated.
256 devices in a mesh: row: 32 (over x, z_hi, y), col: 8 (over z_lo, core).
Axes of the slice: x: 4, y: 4, z: 8 (z_hi: 2, z_lo: 4; z = z_hi * 4 + z_lo), core: 2. Of those that a mesh axis runs over, the one named last changes fastest.
Arguments:
- coupling: float32 [24576, 24576], P('row', 'col'), may hold values from -1 to 5, as said below
- vectors: float32 [24576, 256], P(('row', 'col')), may hold values from -6 to 6
Outputs:
- filtered: float32 [24576, 256], P(('row', 'col'))
- gram: float32 [256, 256], replicated
Inputs may be any that keep to these rules, and one draw needn't show every extreme that they name: `coupling`: H, the operator with its column order restored, is symmetric.
All inputs are finite; a program needn't handle non-finite values.
Results may differ from a plain program's by a relative error of at most 0.0001.
Values sent between devices are 32-bit elements; how exact they have to be, the bound alone decides.
No kernel may reach another device: no remote copies, remote signals or barrier semaphores. Data moves between devices by JAX's collectives and lax.ppermute only.
A program may use at most 64 MiB of HBM per device.

v0:
```python
import functools

import jax
import jax.numpy as jnp
from jax import lax
from jax.experimental import pallas as pl
from jax.experimental.pallas import tpu as pltpu
from jax.sharding import Mesh, PartitionSpec as P


ORDER = 24576
VECS = 256
DEGREE = 6
SH = 96
LOCAL = 768
COLS = 3072

filter_center = 2.75
filter_half = 1.75
filter_lower = 0.0


AX = ("x", "zh", "y", "zl", "core")
DIMS = (4, 2, 4, 4, 2)


def lin(x, zh, y, zl, core):
    return (((x * 2 + zh) * 4 + y) * 4 + zl) * 2 + core


def pairs(move):
    out = []
    for x in range(4):
        for zh in range(2):
            for y in range(4):
                for zl in range(4):
                    for core in range(2):
                        out.append((lin(x, zh, y, zl, core), lin(*move(x, zh, y, zl, core))))
    return out


SWAP_CORE = pairs(lambda x, zh, y, zl, core: (x, zh, y, zl, 1 - core))
SWAP_ZH = pairs(lambda x, zh, y, zl, core: (x, 1 - zh, y, zl, core))


def along_y(x, zh, y, zl, core, s):
    return (x, zh, (y + s) % 4, zl, core)


def along_x(x, zh, y, zl, core, s):
    return ((x + s) % 4, zh, y, zl, core)


FIRST = [pairs(lambda x, zh, y, zl, core, s=s: (along_x if core else along_y)(x, zh, y, zl, core, s)) for s in range(4)]
SECOND = [pairs(lambda x, zh, y, zl, core, s=s: (along_y if core else along_x)(x, zh, y, zl, core, s)) for s in range(4)]
ALONG_ZL = [pairs(lambda x, zh, y, zl, core, s=s: (x, zh, y, (zl + s) % 4, core)) for s in range(4)]


def send(value, moves):
    return lax.ppermute(value, AX, moves)


HALF = 4 * SH
BLOCKS = COLS // HALF
DEEP = 3 * HALF


def split_kernel(place, h_ref, out_ref):
    def write(order):
        h = h_ref[...]
        for block in range(BLOCKS):
            part = jnp.concatenate([h[:, i * SH : (i + 1) * SH] for i in order[4 * block : 4 * block + 4]], axis=1)
            hi = part.astype(jnp.bfloat16)
            out_ref[block, :, :HALF] = hi
            out_ref[block, :, HALF : 2 * HALF] = (part - hi.astype(jnp.float32)).astype(jnp.bfloat16)
            out_ref[block, :, 2 * HALF :] = hi

    @pl.when(place[0] == 0)
    def _():
        write(list(range(32)))

    @pl.when(place[0] != 0)
    def _():
        write([(x * 2 + zh) * 4 + y for y in range(4) for zh in range(2) for x in range(4)])


def split_operator(place, coupling):
    return pl.pallas_call(
        split_kernel,
        grid_spec=pltpu.PrefetchScalarGridSpec(
            num_scalar_prefetch=1,
            grid=(LOCAL // 96,),
            in_specs=[pl.BlockSpec((96, COLS), lambda i, p: (i, 0))],
            out_specs=pl.BlockSpec((BLOCKS, 96, DEEP), lambda i, p: (0, i, 0)),
        ),
        out_shape=jax.ShapeDtypeStruct((BLOCKS, LOCAL, DEEP), jnp.bfloat16),
        compiler_params=pltpu.CompilerParams(vmem_limit_bytes=16 << 20),
    )(place, coupling)


def product_kernel(blocks, has_acc, last, *refs):
    place, operator = refs[:2]
    parts, refs = refs[2 : 2 + len(blocks)], refs[2 + len(blocks) :]
    acc_in, refs = (refs[0], refs[1:]) if has_acc else (None, refs)
    outs, rows_of = refs[:-1], refs[-1]
    core, zl, zh, own_u, own_v = (place[i] for i in range(5))
    for b, part in enumerate(parts):
        for s in range(4):
            rows = part[s * SH : (s + 1) * SH, :]
            hi = rows.astype(jnp.bfloat16)
            lo = (rows - hi.astype(jnp.float32)).astype(jnp.bfloat16)
            at = pl.multiple_of(((own_v - s + 4) % 4) * SH, SH)
            rows_of[b, pl.ds(at, SH), :] = lo
            rows_of[b, pl.ds(HALF + at, SH), :] = hi
            rows_of[b, pl.ds(2 * HALF + at, SH), :] = hi
    for half in range(2):
        m = slice(half * LOCAL // 2, (half + 1) * LOCAL // 2)
        acc = acc_in[m, :] if has_acc else None
        for b, (t, z) in enumerate(blocks):
            block = ((own_u - t + 4) % 4) * 2 + (zh + z) % 2
            term = jnp.dot(operator[block, m, :], rows_of[b], preferred_element_type=jnp.float32)
            acc = term if acc is None else acc + term
        if not last:
            outs[0][m, :] = acc
            continue
        keep, give = outs
        for pair in range(2):
            to = pl.multiple_of(((half * 2 + pair - zl + 4) % 4) * SH, SH)
            even, odd = acc[pair * 2 * SH : pair * 2 * SH + SH], acc[pair * 2 * SH + SH : (pair + 1) * 2 * SH]

            @pl.when(core == 0)
            def _():
                keep[pl.ds(to, SH), :] = even
                give[pl.ds(to, SH), :] = odd

            @pl.when(core != 0)
            def _():
                keep[pl.ds(to, SH), :] = odd
                give[pl.ds(to, SH), :] = even


def product(place, operator, parts, acc, last=False):
    vmem = pl.BlockSpec(memory_space=pltpu.VMEM)
    args = [operator, *parts.values()] + ([] if acc is None else [acc])
    shape = [(HALF, VECS)] * 2 if last else [(LOCAL, VECS)]
    out = pl.pallas_call(
        functools.partial(product_kernel, tuple(parts), acc is not None, last),
        in_specs=[pl.BlockSpec(memory_space=pltpu.SMEM)] + [vmem] * len(args),
        out_specs=[vmem] * len(shape),
        out_shape=[jax.ShapeDtypeStruct(a, jnp.float32) for a in shape],
        scratch_shapes=[pltpu.VMEM((len(parts), DEEP, VECS), jnp.bfloat16)],
        compiler_params=pltpu.CompilerParams(vmem_limit_bytes=20 << 20),
    )(place, *args)
    return out if last else out[0]


def on_device(coupling, vectors):
    x, zh, y, zl, core = (lax.axis_index(a) for a in AX)
    own_u, own_v = jnp.where(core == 0, x, y), jnp.where(core == 0, y, x)
    place = jnp.stack([core, zl, zh, own_u, own_v]).astype(jnp.int32)

    operator = split_operator(place, coupling)

    def along_first(rows):
        near = {s: send(rows, FIRST[s]) for s in (2, 1, 3)}
        return jnp.concatenate([rows, near[1], near[2], near[3]], axis=0)

    def along_second(rows):
        return {s: send(rows, SECOND[s]) for s in (2, 1, 3)}

    def apply(current):
        partner = send(current, SWAP_ZH)
        a = along_first(current)
        b = along_first(partner)
        far_a = along_second(a)
        far_b = along_second(b)
        acc = product(place, operator, {(0, 0): a, (0, 1): b}, None)
        acc = product(place, operator, {(t, 0): far_a[t] for t in (1, 3, 2)}, acc)
        acc = product(place, operator, {(t, 1): far_b[t] for t in (1, 3)}, acc)
        keep, give = product(place, operator, {(2, 1): far_b[2]}, acc, last=True)
        total = keep + send(give, SWAP_CORE)
        here = {s: send(total[s * SH : (s + 1) * SH], ALONG_ZL[s]) for s in (2, 1, 3)}
        return (total[:SH] + here[1]) + (here[2] + here[3])

    sigma_first = filter_half / (filter_lower - filter_center)
    gains, losses = [sigma_first / filter_half], [0.0]
    sigma_now = sigma_first
    for _ in range(DEGREE - 1):
        sigma_new = 1.0 / (2.0 / sigma_first - sigma_now)
        gains.append(2.0 * sigma_new / filter_half)
        losses.append(sigma_now * sigma_new)
        sigma_now = sigma_new

    previous, current = vectors, vectors
    for gain, loss in zip(gains, losses):
        applied = apply(current)
        following = gain * (applied - filter_center * current)
        if loss:
            following = following - loss * previous
        previous, current = current, following

    local = jnp.dot(current.T, current, precision=lax.Precision.HIGHEST, preferred_element_type=jnp.float32)
    halves = local.reshape(2, 128, VECS)
    mine = lax.dynamic_index_in_dim(halves, core, 0, keepdims=False)
    other = lax.dynamic_index_in_dim(halves, 1 - core, 0, keepdims=False)
    half = mine + send(other, SWAP_CORE)
    piece = lax.all_to_all(half.reshape(16, 8, VECS), ("x", "y"), 0, 0).sum(axis=0)
    every = lax.all_to_all(jnp.broadcast_to(piece, (8, 8, VECS)), ("zh", "zl"), 0, 0).sum(axis=0) / ORDER
    half = lax.all_to_all(jnp.broadcast_to(every, (16, 8, VECS)), ("x", "y"), 0, 0).reshape(128, VECS)
    other = send(half, SWAP_CORE)
    gram = jnp.concatenate([jnp.where(core == 0, half, other), jnp.where(core == 0, other, half)], axis=0)
    return current, gram


def solution(mesh):
    fine = Mesh(mesh.devices.reshape(DIMS), AX)
    return jax.shard_map(
        on_device,
        mesh=fine,
        in_specs=(P(("x", "zh", "y"), ("zl", "core")), P(AX, None)),
        out_specs=(P(AX, None), P()),
        check_vma=False,
    )
```

profile of v0, /device:TPU:1, one launch (start us, length us, event | category | flops | bytes accessed | tf_op | source)
XLA Modules:
  0.0 397.6 jit_solution(16854021113406367219)
XLA Ops:
  0.6 7.8 %collective-permute-start = (f32[96,256]{1,0:T(8,128)}, f32[96,256]{1,0:T(8,128)S(1)}, u32[]{:S(2)}, u32[]{:S(2)}) collective-permute-start(f32[96,256]{1,0:T(8,128)} %param.3), channel_id=1, source_target_pairs={{0,32},{1,33},{2,34},{3,35},{4,36},{5,37},{6,38},{7,39},{8,40},{9,... | collective-permute-start | bytes 294920 | tf_op jit(solution)/shard_map/ppermute | solution.py:60
  9.7 2.5 collective-permute-start.8
  20.9 3.1 collective-permute-start.2
  24.0 2.5 collective-permute-done.1
  29.1 4.1 %collective-permute-done.3 = f32[96,256]{1,0:T(8,128)S(1)} collective-permute-done((f32[96,256]{1,0:T(8,128)S(1)}, f32[96,256]{1,0:T(8,128)S(1)}, u32[]{:S(2)}, u32[]{:S(2)}) %collective-permute-start.3) | collective-permute-done | bytes 98336 | tf_op jit(solution)/shard_map/ppermute | solution.py:60
  33.7 2.3 collective-permute-start.6
  36.6 3.7 copy-done
  40.3 6.1 %shard_map.41.refs_1_ = bf16[8,768,1152]{2,1,0:T(8,128)(2,1)S(1)} custom-call(s32[5]{0:T(128)S(1)} %stack.23.place.refs_0_, f32[768,3072]{1,0:T(8,128)S(1)} %copy-done), custom_call_target="tpu_custom_call" | custom-call | tf_op jit(solution)/shard_map/pallas_call | solution.py:88
  48.2 2.4 shard_map.43.refs_4_
  61.4 2.3 collective-permute-done.14
  63.6 4.6 %collective-permute-done.15 = f32[96,256]{1,0:T(8,128)S(1)} collective-permute-done((f32[96,256]{1,0:T(8,128)S(1)}, f32[96,256]{1,0:T(8,128)S(1)}, u32[]{:S(2)}, u32[]{:S(2)}) %collective-permute-start.15) | collective-permute-done | bytes 98336 | tf_op jit(solution)/shard_map/ppermute | solution.py:60
  68.3 3.0 collective-permute-start.25
  75.4 2.5 collective-permute-start.28
  82.2 3.6 collective-permute-done.18
  87.3 3.6 collective-permute-done.20
  96.5 2.4 shard_map.47.refs_4_
  98.9 3.6 collective-permute-done.23.refs_3_
  106.4 5.0 %collective-permute-start.30 = (f32[384,256]{1,0:T(8,128)S(1)}, f32[384,256]{1,0:T(8,128)S(1)}, u32[]{:S(2)}, u32[]{:S(2)}) collective-permute-start(f32[384,256]{1,0:T(8,128)S(1)} %get-tuple-element.17), channel_id=1, source_target_pairs={{0,1},{1,0},{2,3},{3,2},{4,5},{5,4},{6,7},{7,6},{8,9},{9,8},{10,11... | collective-permute-start | bytes 1179656 | tf_op jit(solution)/shard_map/ppermute | solution.py:60
  112.8 2.7 collective-permute-start.31
  118.7 4.9 %collective-permute-done.32 = f32[96,256]{1,0:T(8,128)S(1)} collective-permute-done((f32[96,256]{1,0:T(8,128)S(1)}, f32[96,256]{1,0:T(8,128)S(1)}, u32[]{:S(2)}, u32[]{:S(2)}) %collective-permute-start.32) | collective-permute-done | bytes 98336 | tf_op jit(solution)/shard_map/ppermute | solution.py:60
  124.4 3.9 collective-permute-start.42
  132.1 2.7 collective-permute-start.45
  134.8 2.5 collective-permute-done.34
  138.3 3.9 collective-permute-done.35
  144.3 2.7 collective-permute-done.37
  152.4 2.4 shard_map.51.refs_4_
  157.1 2.9 collective-permute-done.38.refs_2_
  161.9 7.8 %collective-permute-start.47 = (f32[384,256]{1,0:T(8,128)S(1)}, f32[384,256]{1,0:T(8,128)S(1)}, u32[]{:S(2)}, u32[]{:S(2)}) collective-permute-start(f32[384,256]{1,0:T(8,128)S(1)} %get-tuple-element.19), channel_id=1, source_target_pairs={{0,1},{1,0},{2,3},{3,2},{4,5},{5,4},{6,7},{7,6},{8,9},{9,8},{10,11... | collective-permute-start | bytes 1179656 | tf_op jit(solution)/shard_map/ppermute | solution.py:60
  171.2 2.2 collective-permute-start.48
  177.0 4.9 %collective-permute-done.49 = f32[96,256]{1,0:T(8,128)S(1)} collective-permute-done((f32[96,256]{1,0:T(8,128)S(1)}, f32[96,256]{1,0:T(8,128)S(1)}, u32[]{:S(2)}, u32[]{:S(2)}) %collective-permute-start.49) | collective-permute-done | bytes 98336 | tf_op jit(solution)/shard_map/ppermute | solution.py:60
  182.3 4.1 %collective-permute-start.59 = (f32[96,256]{1,0:T(8,128)S(1)}, f32[96,256]{1,0:T(8,128)S(1)}, u32[]{:S(2)}, u32[]{:S(2)}) collective-permute-start(f32[96,256]{1,0:T(8,128)S(1)} %fusion.16), channel_id=1, source_target_pairs={{0,16},{1,129},{2,18},{3,131},{4,20},{5,133},{6,22},{7,135},{8,24}... | collective-permute-start | bytes 294920 | tf_op jit(solution)/shard_map/ppermute | solution.py:60
  190.3 2.7 collective-permute-start.62
  193.0 2.7 collective-permute-done.51
  196.5 4.8 %collective-permute-done.52 = f32[96,256]{1,0:T(8,128)S(1)} collective-permute-done((f32[96,256]{1,0:T(8,128)S(1)}, f32[96,256]{1,0:T(8,128)S(1)}, u32[]{:S(2)}, u32[]{:S(2)}) %collective-permute-start.52) | collective-permute-done | bytes 98336 | tf_op jit(solution)/shard_map/ppermute | solution.py:60
  202.0 3.0 collective-permute-done.54
  205.5 2.3 collective-permute-start.57
  209.9 2.4 shard_map.55.refs_4_
  215.0 2.5 collective-permute-done.55.refs_2_
  219.4 8.6 %collective-permute-start.64 = (f32[384,256]{1,0:T(8,128)S(1)}, f32[384,256]{1,0:T(8,128)S(1)}, u32[]{:S(2)}, u32[]{:S(2)}) collective-permute-start(f32[384,256]{1,0:T(8,128)S(1)} %get-tuple-element.21), channel_id=1, source_target_pairs={{0,1},{1,0},{2,3},{3,2},{4,5},{5,4},{6,7},{7,6},{8,9},{9,8},{10,11... | collective-permute-start | bytes 1179656 | tf_op jit(solution)/shard_map/ppermute | solution.py:60
  235.7 5.0 %collective-permute-done.66 = f32[96,256]{1,0:T(8,128)S(1)} collective-permute-done((f32[96,256]{1,0:T(8,128)S(1)}, f32[96,256]{1,0:T(8,128)S(1)}, u32[]{:S(2)}, u32[]{:S(2)}) %collective-permute-start.66) | collective-permute-done | bytes 98336 | tf_op jit(solution)/shard_map/ppermute | solution.py:60
  240.8 4.1 %collective-permute-start.76 = (f32[96,256]{1,0:T(8,128)S(1)}, f32[96,256]{1,0:T(8,128)S(1)}, u32[]{:S(2)}, u32[]{:S(2)}) collective-permute-start(f32[96,256]{1,0:T(8,128)S(1)} %fusion.12), channel_id=1, source_target_pairs={{0,16},{1,129},{2,18},{3,131},{4,20},{5,133},{6,22},{7,135},{8,24}... | collective-permute-start | bytes 294920 | tf_op jit(solution)/shard_map/ppermute | solution.py:60
  248.8 2.7 collective-permute-start.79
  251.4 2.9 collective-permute-done.68
  254.6 5.1 %collective-permute-done.69 = f32[96,256]{1,0:T(8,128)S(1)} collective-permute-done((f32[96,256]{1,0:T(8,128)S(1)}, f32[96,256]{1,0:T(8,128)S(1)}, u32[]{:S(2)}, u32[]{:S(2)}) %collective-permute-start.69) | collective-permute-done | bytes 98336 | tf_op jit(solution)/shard_map/ppermute | solution.py:60
  260.6 2.9 collective-permute-done.71
  263.7 2.6 collective-permute-start.74
  268.4 2.4 shard_map.59.refs_4_
  271.4 3.8 collective-permute-done.74.refs_3_
  279.0 7.4 %collective-permute-start.81 = (f32[384,256]{1,0:T(8,128)S(1)}, f32[384,256]{1,0:T(8,128)S(1)}, u32[]{:S(2)}, u32[]{:S(2)}) collective-permute-start(f32[384,256]{1,0:T(8,128)S(1)} %get-tuple-element.23), channel_id=1, source_target_pairs={{0,1},{1,0},{2,3},{3,2},{4,5},{5,4},{6,7},{7,6},{8,9},{9,8},{10,11... | collective-permute-start | bytes 1179656 | tf_op jit(solution)/shard_map/ppermute | solution.py:60
  293.7 4.9 %collective-permute-done.83 = f32[96,256]{1,0:T(8,128)S(1)} collective-permute-done((f32[96,256]{1,0:T(8,128)S(1)}, f32[96,256]{1,0:T(8,128)S(1)}, u32[]{:S(2)}, u32[]{:S(2)}) %collective-permute-start.83) | collective-permute-done | bytes 98336 | tf_op jit(solution)/shard_map/ppermute | solution.py:60
  298.8 4.1 %collective-permute-start.93 = (f32[96,256]{1,0:T(8,128)S(1)}, f32[96,256]{1,0:T(8,128)S(1)}, u32[]{:S(2)}, u32[]{:S(2)}) collective-permute-start(f32[96,256]{1,0:T(8,128)S(1)} %fusion.8), channel_id=1, source_target_pairs={{0,16},{1,129},{2,18},{3,131},{4,20},{5,133},{6,22},{7,135},{8,24}... | collective-permute-start | bytes 294920 | tf_op jit(solution)/shard_map/ppermute | solution.py:60
  306.8 2.7 collective-permute-start.96
  309.5 2.7 collective-permute-done.85
  312.5 5.3 %collective-permute-done.86 = f32[96,256]{1,0:T(8,128)S(1)} collective-permute-done((f32[96,256]{1,0:T(8,128)S(1)}, f32[96,256]{1,0:T(8,128)S(1)}, u32[]{:S(2)}, u32[]{:S(2)}) %collective-permute-start.86) | collective-permute-done | bytes 98336 | tf_op jit(solution)/shard_map/ppermute | solution.py:60
  318.5 3.2 collective-permute-done.88
  326.6 2.4 shard_map.63.refs_4_
  335.9 8.1 %collective-permute-start.98 = (f32[384,256]{1,0:T(8,128)S(1)}, f32[384,256]{1,0:T(8,128)S(1)}, u32[]{:S(2)}, u32[]{:S(2)}) collective-permute-start(f32[384,256]{1,0:T(8,128)S(1)} %get-tuple-element.25), channel_id=1, source_target_pairs={{0,1},{1,0},{2,3},{3,2},{4,5},{5,4},{6,7},{7,6},{8,9},{9,8},{10,11... | collective-permute-start | bytes 1179656 | tf_op jit(solution)/shard_map/ppermute | solution.py:60
  346.6 3.1 collective-permute-start.101
  350.4 2.8 collective-permute-done.101
  353.2 3.5 collective-permute-done.99
  359.4 11.4 %all_to_all.15 = f32[16,8,256]{2,1,0:T(8,128)S(1)} all-to-all(f32[16,8,256]{2,1,0:T(8,128)S(1)} %fusion), channel_id=1, replica_groups=mesh['x'=4,'zh'=2,'y'=4,'zl'=4,'core'=2] {'x','y'}, dimensions={0} | all-to-all | bytes 262144 | tf_op jit(solution)/shard_map/all_to_all | solution.py:207
  370.8 10.3 %all_to_all.16 = f32[8,8,256]{2,1,0:T(8,128)S(1)} all-to-all(f32[8,8,256]{2,1,0:T(8,128)S(1)} %broadcast_in_dim.6), channel_id=1, replica_groups=mesh['x'=4,'zh'=2,'y'=4,'zl'=4,'core'=2] {'zh','zl'}, dimensions={0} | all-to-all | bytes 131072 | tf_op jit(solution)/shard_map/all_to_all | solution.py:208
  381.2 10.2 %all_to_all.17 = f32[16,8,256]{2,1,0:T(8,128)S(1)} all-to-all(f32[16,8,256]{2,1,0:T(8,128)S(1)} %broadcast_in_dim.7), channel_id=1, replica_groups=mesh['x'=4,'zh'=2,'y'=4,'zl'=4,'core'=2] {'x','y'}, dimensions={0} | all-to-all | bytes 262144 | tf_op jit(solution)/shard_map/all_to_all | solution.py:209
  391.4 4.3 %collective-permute-start.103 = (f32[128,256]{1,0:T(8,128)S(1)}, f32[128,256]{1,0:T(8,128)S(1)}, u32[]{:S(2)}, u32[]{:S(2)}) collective-permute-start(f32[128,256]{1,0:T(8,128)S(1)} %bitcast.21), channel_id=1, source_target_pairs={{0,1},{1,0},{2,3},{3,2},{4,5},{5,4},{6,7},{7,6},{8,9},{9,8},{10,11... | collective-permute-start | bytes 393224 | tf_op jit(solution)/shard_map/ppermute | solution.py:60
  (240 shorter events, 136.5 us)
Async XLA Ops:
  0.6 19.9 %collective-permute-start = (f32[96,256]{1,0:T(8,128)}, f32[96,256]{1,0:T(8,128)S(1)}, u32[]{:S(2)}, u32[]{:S(2)}) collective-permute-start(f32[96,256]{1,0:T(8,128)} %param.3), channel_id=1, source_target_pairs={{0,32},{1,33},{2,34},{3,35},{4,36},{5,37},{6,38},{7,39},{8,40},{9,... | collective-permute-start | bytes 294920 | tf_op jit(solution)/shard_map/ppermute | solution.py:60
  15.8 20.2 %collective-permute-start.10 = (f32[384,256]{1,0:T(8,128)S(1)}, f32[384,256]{1,0:T(8,128)S(1)}, u32[]{:S(2)}, u32[]{:S(2)}) collective-permute-start(f32[384,256]{1,0:T(8,128)S(1)} %constant_dynamic-update-slice_fusion.4.refs_2_), channel_id=1, source_target_pairs={{0,64},{1,9},{2,66},{3,11},{4,68},{5,13},{6,70},{7,15},{8,72},{9,1... | collective-permute-start | bytes 1179656 | tf_op jit(solution)/shard_map/ppermute | solution.py:60
  17.5 30.8 %collective-permute-start.11 = (f32[384,256]{1,0:T(8,128)S(1)}, f32[384,256]{1,0:T(8,128)S(1)}, u32[]{:S(2)}, u32[]{:S(2)}) collective-permute-start(f32[384,256]{1,0:T(8,128)S(1)} %constant_dynamic-update-slice_fusion.4.refs_2_), channel_id=1, source_target_pairs={{0,192},{1,25},{2,194},{3,27},{4,196},{5,29},{6,198},{7,31},{8,200... | collective-permute-start | bytes 1179656 | tf_op jit(solution)/shard_map/ppermute | solution.py:60
  18.7 29.5 %collective-permute-start.12 = (f32[384,256]{1,0:T(8,128)S(1)}, f32[384,256]{1,0:T(8,128)S(1)}, u32[]{:S(2)}, u32[]{:S(2)}) collective-permute-start(f32[384,256]{1,0:T(8,128)S(1)} %constant_dynamic-update-slice_fusion.4.refs_2_), channel_id=1, source_target_pairs={{0,128},{1,17},{2,130},{3,19},{4,132},{5,21},{6,134},{7,23},{8,136... | collective-permute-start | bytes 1179656 | tf_op jit(solution)/shard_map/ppermute | solution.py:60
  20.9 8.2 %collective-permute-start.2 = (f32[96,256]{1,0:T(8,128)S(1)}, f32[96,256]{1,0:T(8,128)S(1)}, u32[]{:S(2)}, u32[]{:S(2)}) collective-permute-start(f32[96,256]{1,0:T(8,128)S(1)} %collective-permute-done), channel_id=1, source_target_pairs={{0,16},{1,129},{2,18},{3,131},{4,20},{5,133},{6,22},{7,135},{8,24}... | collective-permute-start | bytes 294920 | tf_op jit(solution)/shard_map/ppermute | solution.py:60
  26.6 6.7 %collective-permute-start.3 = (f32[96,256]{1,0:T(8,128)S(1)}, f32[96,256]{1,0:T(8,128)S(1)}, u32[]{:S(2)}, u32[]{:S(2)}) collective-permute-start(f32[96,256]{1,0:T(8,128)S(1)} %collective-permute-done), channel_id=1, source_target_pairs={{0,24},{1,193},{2,26},{3,195},{4,28},{5,197},{6,30},{7,199},{8,0},... | collective-permute-start | bytes 294920 | tf_op jit(solution)/shard_map/ppermute | solution.py:60
  33.3 17.4 %collective-permute-start.5 = (f32[384,256]{1,0:T(8,128)S(1)}, f32[384,256]{1,0:T(8,128)S(1)}, u32[]{:S(2)}, u32[]{:S(2)}) collective-permute-start(f32[384,256]{1,0:T(8,128)S(1)} %constant_dynamic-update-slice_fusion.refs_3_), channel_id=1, source_target_pairs={{0,64},{1,9},{2,66},{3,11},{4,68},{5,13},{6,70},{7,15},{8,72},{9,1... | collective-permute-start | bytes 1179656 | tf_op jit(solution)/shard_map/ppermute | solution.py:60
  33.7 16.9 %collective-permute-start.6 = (f32[384,256]{1,0:T(8,128)S(1)}, f32[384,256]{1,0:T(8,128)S(1)}, u32[]{:S(2)}, u32[]{:S(2)}) collective-permute-start(f32[384,256]{1,0:T(8,128)S(1)} %constant_dynamic-update-slice_fusion.refs_3_), channel_id=1, source_target_pairs={{0,192},{1,25},{2,194},{3,27},{4,196},{5,29},{6,198},{7,31},{8,200... | collective-permute-start | bytes 1179656 | tf_op jit(solution)/shard_map/ppermute | solution.py:60
  36.0 16.5 %collective-permute-start.4 = (f32[384,256]{1,0:T(8,128)S(1)}, f32[384,256]{1,0:T(8,128)S(1)}, u32[]{:S(2)}, u32[]{:S(2)}) collective-permute-start(f32[384,256]{1,0:T(8,128)S(1)} %constant_dynamic-update-slice_fusion.refs_3_), channel_id=1, source_target_pairs={{0,128},{1,17},{2,130},{3,19},{4,132},{5,21},{6,134},{7,23},{8,136... | collective-permute-start | bytes 1179656 | tf_op jit(solution)/shard_map/ppermute | solution.py:60
  58.5 9.7 %collective-permute-start.15 = (f32[96,256]{1,0:T(8,128)S(1)}, f32[96,256]{1,0:T(8,128)S(1)}, u32[]{:S(2)}, u32[]{:S(2)}) collective-permute-start(f32[96,256]{1,0:T(8,128)S(1)} %get-tuple-element.45), channel_id=1, source_target_pairs={{0,4},{1,5},{2,6},{3,7},{4,0},{5,1},{6,2},{7,3},{8,12},{9,13},{10,... | collective-permute-start | bytes 294920 | tf_op jit(solution)/shard_map/ppermute | solution.py:60
  59.7 8.5 %collective-permute-start.16 = (f32[96,256]{1,0:T(8,128)S(1)}, f32[96,256]{1,0:T(8,128)S(1)}, u32[]{:S(2)}, u32[]{:S(2)}) collective-permute-start(f32[96,256]{1,0:T(8,128)S(1)} %get-tuple-element.44), channel_id=1, source_target_pairs={{0,6},{1,7},{2,0},{3,1},{4,2},{5,3},{6,4},{7,5},{8,14},{9,15},{10,... | collective-permute-start | bytes 294920 | tf_op jit(solution)/shard_map/ppermute | solution.py:60
  71.5 7.7 %collective-permute-start.17 = (f32[96,256]{1,0:T(8,128)S(1)}, f32[96,256]{1,0:T(8,128)S(1)}, u32[]{:S(2)}, u32[]{:S(2)}) collective-permute-start(f32[96,256]{1,0:T(8,128)S(1)} %get-tuple-element.26), channel_id=1, source_target_pairs={{0,32},{1,33},{2,34},{3,35},{4,36},{5,37},{6,38},{7,39},{8,40},{9,... | collective-permute-start | bytes 294920 | tf_op jit(solution)/shard_map/ppermute | solution.py:60
  75.1 18.5 %collective-permute-start.27 = (f32[384,256]{1,0:T(8,128)S(1)}, f32[384,256]{1,0:T(8,128)S(1)}, u32[]{:S(2)}, u32[]{:S(2)}) collective-permute-start(f32[384,256]{1,0:T(8,128)S(1)} %pad_maximum_fusion.refs_2_), channel_id=1, source_target_pairs={{0,64},{1,9},{2,66},{3,11},{4,68},{5,13},{6,70},{7,15},{8,72},{9,1... | collective-permute-start | bytes 1179656 | tf_op jit(solution)/shard_map/ppermute | solution.py:60
  75.4 21.2 %collective-permute-start.28 = (f32[384,256]{1,0:T(8,128)S(1)}, f32[384,256]{1,0:T(8,128)S(1)}, u32[]{:S(2)}, u32[]{:S(2)}) collective-permute-start(f32[384,256]{1,0:T(8,128)S(1)} %pad_maximum_fusion.refs_2_), channel_id=1, source_target_pairs={{0,192},{1,25},{2,194},{3,27},{4,196},{5,29},{6,198},{7,31},{8,200... | collective-permute-start | bytes 1179656 | tf_op jit(solution)/shard_map/ppermute | solution.py:60
  77.9 18.7 %collective-permute-start.29 = (f32[384,256]{1,0:T(8,128)S(1)}, f32[384,256]{1,0:T(8,128)S(1)}, u32[]{:S(2)}, u32[]{:S(2)}) collective-permute-start(f32[384,256]{1,0:T(8,128)S(1)} %pad_maximum_fusion.refs_2_), channel_id=1, source_target_pairs={{0,128},{1,17},{2,130},{3,19},{4,132},{5,21},{6,134},{7,23},{8,136... | collective-permute-start | bytes 1179656 | tf_op jit(solution)/shard_map/ppermute | solution.py:60
  80.6 6.6 %collective-permute-start.19 = (f32[96,256]{1,0:T(8,128)S(1)}, f32[96,256]{1,0:T(8,128)S(1)}, u32[]{:S(2)}, u32[]{:S(2)}) collective-permute-start(f32[96,256]{1,0:T(8,128)S(1)} %collective-permute-done.17), channel_id=1, source_target_pairs={{0,16},{1,129},{2,18},{3,131},{4,20},{5,133},{6,22},{7,135},{8,24}... | collective-permute-start | bytes 294920 | tf_op jit(solution)/shard_map/ppermute | solution.py:60
  90.9 8.1 %collective-permute-start.22 = (f32[384,256]{1,0:T(8,128)S(1)}, f32[384,256]{1,0:T(8,128)S(1)}, u32[]{:S(2)}, u32[]{:S(2)}) collective-permute-start(f32[384,256]{1,0:T(8,128)S(1)} %constant_dynamic-update-slice_fusion.8.refs_3_), channel_id=1, source_target_pairs={{0,64},{1,9},{2,66},{3,11},{4,68},{5,13},{6,70},{7,15},{8,72},{9,1... | collective-permute-start | bytes 1179656 | tf_op jit(solution)/shard_map/ppermute | solution.py:60
  92.0 10.5 %collective-permute-start.23 = (f32[384,256]{1,0:T(8,128)S(1)}, f32[384,256]{1,0:T(8,128)S(1)}, u32[]{:S(2)}, u32[]{:S(2)}) collective-permute-start(f32[384,256]{1,0:T(8,128)S(1)} %constant_dynamic-update-slice_fusion.8.refs_3_), channel_id=1, source_target_pairs={{0,192},{1,25},{2,194},{3,27},{4,196},{5,29},{6,198},{7,31},{8,200... | collective-permute-start | bytes 1179656 | tf_op jit(solution)/shard_map/ppermute | solution.py:60
  93.6 10.8 %collective-permute-start.21 = (f32[384,256]{1,0:T(8,128)S(1)}, f32[384,256]{1,0:T(8,128)S(1)}, u32[]{:S(2)}, u32[]{:S(2)}) collective-permute-start(f32[384,256]{1,0:T(8,128)S(1)} %constant_dynamic-update-slice_fusion.8.refs_3_), channel_id=1, source_target_pairs={{0,128},{1,17},{2,130},{3,19},{4,132},{5,21},{6,134},{7,23},{8,136... | collective-permute-start | bytes 1179656 | tf_op jit(solution)/shard_map/ppermute | solution.py:60
  115.5 8.1 %collective-permute-start.32 = (f32[96,256]{1,0:T(8,128)S(1)}, f32[96,256]{1,0:T(8,128)S(1)}, u32[]{:S(2)}, u32[]{:S(2)}) collective-permute-start(f32[96,256]{1,0:T(8,128)S(1)} %get-tuple-element.41), channel_id=1, source_target_pairs={{0,4},{1,5},{2,6},{3,7},{4,0},{5,1},{6,2},{7,3},{8,12},{9,13},{10,... | collective-permute-start | bytes 294920 | tf_op jit(solution)/shard_map/ppermute | solution.py:60
  115.7 7.9 %collective-permute-start.33 = (f32[96,256]{1,0:T(8,128)S(1)}, f32[96,256]{1,0:T(8,128)S(1)}, u32[]{:S(2)}, u32[]{:S(2)}) collective-permute-start(f32[96,256]{1,0:T(8,128)S(1)} %get-tuple-element.40), channel_id=1, source_target_pairs={{0,6},{1,7},{2,0},{3,1},{4,2},{5,3},{6,4},{7,5},{8,14},{9,15},{10,... | collective-permute-start | bytes 294920 | tf_op jit(solution)/shard_map/ppermute | solution.py:60
  124.4 7.0 %collective-permute-start.42 = (f32[96,256]{1,0:T(8,128)S(1)}, f32[96,256]{1,0:T(8,128)S(1)}, u32[]{:S(2)}, u32[]{:S(2)}) collective-permute-start(f32[96,256]{1,0:T(8,128)S(1)} %fusion.20), channel_id=1, source_target_pairs={{0,16},{1,129},{2,18},{3,131},{4,20},{5,133},{6,22},{7,135},{8,24}... | collective-permute-start | bytes 294920 | tf_op jit(solution)/shard_map/ppermute | solution.py:60
  128.3 9.0 %collective-permute-start.34 = (f32[96,256]{1,0:T(8,128)S(1)}, f32[96,256]{1,0:T(8,128)S(1)}, u32[]{:S(2)}, u32[]{:S(2)}) collective-permute-start(f32[96,256]{1,0:T(8,128)S(1)} %fusion.20), channel_id=1, source_target_pairs={{0,32},{1,33},{2,34},{3,35},{4,36},{5,37},{6,38},{7,39},{8,40},{9,... | collective-permute-start | bytes 294920 | tf_op jit(solution)/shard_map/ppermute | solution.py:60
  131.8 18.0 %collective-permute-start.44 = (f32[384,256]{1,0:T(8,128)S(1)}, f32[384,256]{1,0:T(8,128)S(1)}, u32[]{:S(2)}, u32[]{:S(2)}) collective-permute-start(f32[384,256]{1,0:T(8,128)S(1)} %pad_maximum_fusion.1.refs_2_), channel_id=1, source_target_pairs={{0,64},{1,9},{2,66},{3,11},{4,68},{5,13},{6,70},{7,15},{8,72},{9,1... | collective-permute-start | bytes 1179656 | tf_op jit(solution)/shard_map/ppermute | solution.py:60
  132.1 20.3 %collective-permute-start.45 = (f32[384,256]{1,0:T(8,128)S(1)}, f32[384,256]{1,0:T(8,128)S(1)}, u32[]{:S(2)}, u32[]{:S(2)}) collective-permute-start(f32[384,256]{1,0:T(8,128)S(1)} %pad_maximum_fusion.1.refs_2_), channel_id=1, source_target_pairs={{0,192},{1,25},{2,194},{3,27},{4,196},{5,29},{6,198},{7,31},{8,200... | collective-permute-start | bytes 1179656 | tf_op jit(solution)/shard_map/ppermute | solution.py:60
  134.8 17.7 %collective-permute-start.46 = (f32[384,256]{1,0:T(8,128)S(1)}, f32[384,256]{1,0:T(8,128)S(1)}, u32[]{:S(2)}, u32[]{:S(2)}) collective-permute-start(f32[384,256]{1,0:T(8,128)S(1)} %pad_maximum_fusion.1.refs_2_), channel_id=1, source_target_pairs={{0,128},{1,17},{2,130},{3,19},{4,132},{5,21},{6,134},{7,23},{8,136... | collective-permute-start | bytes 1179656 | tf_op jit(solution)/shard_map/ppermute | solution.py:60
  147.0 7.9 %collective-permute-start.39 = (f32[384,256]{1,0:T(8,128)S(1)}, f32[384,256]{1,0:T(8,128)S(1)}, u32[]{:S(2)}, u32[]{:S(2)}) collective-permute-start(f32[384,256]{1,0:T(8,128)S(1)} %constant_dynamic-update-slice_fusion.12.refs_3_), channel_id=1, source_target_pairs={{0,64},{1,9},{2,66},{3,11},{4,68},{5,13},{6,70},{7,15},{8,72},{9,1... | collective-permute-start | bytes 1179656 | tf_op jit(solution)/shard_map/ppermute | solution.py:60
  147.7 7.5 %collective-permute-start.40 = (f32[384,256]{1,0:T(8,128)S(1)}, f32[384,256]{1,0:T(8,128)S(1)}, u32[]{:S(2)}, u32[]{:S(2)}) collective-permute-start(f32[384,256]{1,0:T(8,128)S(1)} %constant_dynamic-update-slice_fusion.12.refs_3_), channel_id=1, source_target_pairs={{0,192},{1,25},{2,194},{3,27},{4,196},{5,29},{6,198},{7,31},{8,200... | collective-permute-start | bytes 1179656 | tf_op jit(solution)/shard_map/ppermute | solution.py:60
  149.8 10.2 %collective-permute-start.38 = (f32[384,256]{1,0:T(8,128)S(1)}, f32[384,256]{1,0:T(8,128)S(1)}, u32[]{:S(2)}, u32[]{:S(2)}) collective-permute-start(f32[384,256]{1,0:T(8,128)S(1)} %constant_dynamic-update-slice_fusion.12.refs_3_), channel_id=1, source_target_pairs={{0,128},{1,17},{2,130},{3,19},{4,132},{5,21},{6,134},{7,23},{8,136... | collective-permute-start | bytes 1179656 | tf_op jit(solution)/shard_map/ppermute | solution.py:60
  161.9 9.1 %collective-permute-start.47 = (f32[384,256]{1,0:T(8,128)S(1)}, f32[384,256]{1,0:T(8,128)S(1)}, u32[]{:S(2)}, u32[]{:S(2)}) collective-permute-start(f32[384,256]{1,0:T(8,128)S(1)} %get-tuple-element.19), channel_id=1, source_target_pairs={{0,1},{1,0},{2,3},{3,2},{4,5},{5,4},{6,7},{7,6},{8,9},{9,8},{10,11... | collective-permute-start | bytes 1179656 | tf_op jit(solution)/shard_map/ppermute | solution.py:60
  173.4 8.6 %collective-permute-start.49 = (f32[96,256]{1,0:T(8,128)S(1)}, f32[96,256]{1,0:T(8,128)S(1)}, u32[]{:S(2)}, u32[]{:S(2)}) collective-permute-start(f32[96,256]{1,0:T(8,128)S(1)} %get-tuple-element.38), channel_id=1, source_target_pairs={{0,4},{1,5},{2,6},{3,7},{4,0},{5,1},{6,2},{7,3},{8,12},{9,13},{10,... | collective-permute-start | bytes 294920 | tf_op jit(solution)/shard_map/ppermute | solution.py:60
  174.0 8.0 %collective-permute-start.50 = (f32[96,256]{1,0:T(8,128)S(1)}, f32[96,256]{1,0:T(8,128)S(1)}, u32[]{:S(2)}, u32[]{:S(2)}) collective-permute-start(f32[96,256]{1,0:T(8,128)S(1)} %get-tuple-element.37), channel_id=1, source_target_pairs={{0,6},{1,7},{2,0},{3,1},{4,2},{5,3},{6,4},{7,5},{8,14},{9,15},{10,... | collective-permute-start | bytes 294920 | tf_op jit(solution)/shard_map/ppermute | solution.py:60
  182.3 7.2 %collective-permute-start.59 = (f32[96,256]{1,0:T(8,128)S(1)}, f32[96,256]{1,0:T(8,128)S(1)}, u32[]{:S(2)}, u32[]{:S(2)}) collective-permute-start(f32[96,256]{1,0:T(8,128)S(1)} %fusion.16), channel_id=1, source_target_pairs={{0,16},{1,129},{2,18},{3,131},{4,20},{5,133},{6,22},{7,135},{8,24}... | collective-permute-start | bytes 294920 | tf_op jit(solution)/shard_map/ppermute | solution.py:60
  186.5 9.3 %collective-permute-start.51 = (f32[96,256]{1,0:T(8,128)S(1)}, f32[96,256]{1,0:T(8,128)S(1)}, u32[]{:S(2)}, u32[]{:S(2)}) collective-permute-start(f32[96,256]{1,0:T(8,128)S(1)} %fusion.16), channel_id=1, source_target_pairs={{0,32},{1,33},{2,34},{3,35},{4,36},{5,37},{6,38},{7,39},{8,40},{9,... | collective-permute-start | bytes 294920 | tf_op jit(solution)/shard_map/ppermute | solution.py:60
  190.2 17.5 %collective-permute-start.61 = (f32[384,256]{1,0:T(8,128)S(1)}, f32[384,256]{1,0:T(8,128)S(1)}, u32[]{:S(2)}, u32[]{:S(2)}) collective-permute-start(f32[384,256]{1,0:T(8,128)S(1)} %pad_maximum_fusion.2.refs_2_), channel_id=1, source_target_pairs={{0,64},{1,9},{2,66},{3,11},{4,68},{5,13},{6,70},{7,15},{8,72},{9,1... | collective-permute-start | bytes 1179656 | tf_op jit(solution)/shard_map/ppermute | solution.py:60
  190.3 19.5 %collective-permute-start.62 = (f32[384,256]{1,0:T(8,128)S(1)}, f32[384,256]{1,0:T(8,128)S(1)}, u32[]{:S(2)}, u32[]{:S(2)}) collective-permute-start(f32[384,256]{1,0:T(8,128)S(1)} %pad_maximum_fusion.2.refs_2_), channel_id=1, source_target_pairs={{0,192},{1,25},{2,194},{3,27},{4,196},{5,29},{6,198},{7,31},{8,200... | collective-permute-start | bytes 1179656 | tf_op jit(solution)/shard_map/ppermute | solution.py:60
  193.0 16.9 %collective-permute-start.63 = (f32[384,256]{1,0:T(8,128)S(1)}, f32[384,256]{1,0:T(8,128)S(1)}, u32[]{:S(2)}, u32[]{:S(2)}) collective-permute-start(f32[384,256]{1,0:T(8,128)S(1)} %pad_maximum_fusion.2.refs_2_), channel_id=1, source_target_pairs={{0,128},{1,17},{2,130},{3,19},{4,132},{5,21},{6,134},{7,23},{8,136... | collective-permute-start | bytes 1179656 | tf_op jit(solution)/shard_map/ppermute | solution.py:60
  205.0 7.9 %collective-permute-start.56 = (f32[384,256]{1,0:T(8,128)S(1)}, f32[384,256]{1,0:T(8,128)S(1)}, u32[]{:S(2)}, u32[]{:S(2)}) collective-permute-start(f32[384,256]{1,0:T(8,128)S(1)} %constant_dynamic-update-slice_fusion.16.refs_3_), channel_id=1, source_target_pairs={{0,64},{1,9},{2,66},{3,11},{4,68},{5,13},{6,70},{7,15},{8,72},{9,1... | collective-permute-start | bytes 1179656 | tf_op jit(solution)/shard_map/ppermute | solution.py:60
  205.5 7.7 %collective-permute-start.57 = (f32[384,256]{1,0:T(8,128)S(1)}, f32[384,256]{1,0:T(8,128)S(1)}, u32[]{:S(2)}, u32[]{:S(2)}) collective-permute-start(f32[384,256]{1,0:T(8,128)S(1)} %constant_dynamic-update-slice_fusion.16.refs_3_), channel_id=1, source_target_pairs={{0,192},{1,25},{2,194},{3,27},{4,196},{5,29},{6,198},{7,31},{8,200... | collective-permute-start | bytes 1179656 | tf_op jit(solution)/shard_map/ppermute | solution.py:60
  207.8 9.6 %collective-permute-start.55 = (f32[384,256]{1,0:T(8,128)S(1)}, f32[384,256]{1,0:T(8,128)S(1)}, u32[]{:S(2)}, u32[]{:S(2)}) collective-permute-start(f32[384,256]{1,0:T(8,128)S(1)} %constant_dynamic-update-slice_fusion.16.refs_3_), channel_id=1, source_target_pairs={{0,128},{1,17},{2,130},{3,19},{4,132},{5,21},{6,134},{7,23},{8,136... | collective-permute-start | bytes 1179656 | tf_op jit(solution)/shard_map/ppermute | solution.py:60
  219.4 9.9 %collective-permute-start.64 = (f32[384,256]{1,0:T(8,128)S(1)}, f32[384,256]{1,0:T(8,128)S(1)}, u32[]{:S(2)}, u32[]{:S(2)}) collective-permute-start(f32[384,256]{1,0:T(8,128)S(1)} %get-tuple-element.21), channel_id=1, source_target_pairs={{0,1},{1,0},{2,3},{3,2},{4,5},{5,4},{6,7},{7,6},{8,9},{9,8},{10,11... | collective-permute-start | bytes 1179656 | tf_op jit(solution)/shard_map/ppermute | solution.py:60
  231.4 9.3 %collective-permute-start.66 = (f32[96,256]{1,0:T(8,128)S(1)}, f32[96,256]{1,0:T(8,128)S(1)}, u32[]{:S(2)}, u32[]{:S(2)}) collective-permute-start(f32[96,256]{1,0:T(8,128)S(1)} %get-tuple-element.35), channel_id=1, source_target_pairs={{0,4},{1,5},{2,6},{3,7},{4,0},{5,1},{6,2},{7,3},{8,12},{9,13},{10,... | collective-permute-start | bytes 294920 | tf_op jit(solution)/shard_map/ppermute | solution.py:60
  232.7 7.9 %collective-permute-start.67 = (f32[96,256]{1,0:T(8,128)S(1)}, f32[96,256]{1,0:T(8,128)S(1)}, u32[]{:S(2)}, u32[]{:S(2)}) collective-permute-start(f32[96,256]{1,0:T(8,128)S(1)} %get-tuple-element.34), channel_id=1, source_target_pairs={{0,6},{1,7},{2,0},{3,1},{4,2},{5,3},{6,4},{7,5},{8,14},{9,15},{10,... | collective-permute-start | bytes 294920 | tf_op jit(solution)/shard_map/ppermute | solution.py:60
  240.8 7.2 %collective-permute-start.76 = (f32[96,256]{1,0:T(8,128)S(1)}, f32[96,256]{1,0:T(8,128)S(1)}, u32[]{:S(2)}, u32[]{:S(2)}) collective-permute-start(f32[96,256]{1,0:T(8,128)S(1)} %fusion.12), channel_id=1, source_target_pairs={{0,16},{1,129},{2,18},{3,131},{4,20},{5,133},{6,22},{7,135},{8,24}... | collective-permute-start | bytes 294920 | tf_op jit(solution)/shard_map/ppermute | solution.py:60
  244.9 9.4 %collective-permute-start.68 = (f32[96,256]{1,0:T(8,128)S(1)}, f32[96,256]{1,0:T(8,128)S(1)}, u32[]{:S(2)}, u32[]{:S(2)}) collective-permute-start(f32[96,256]{1,0:T(8,128)S(1)} %fusion.12), channel_id=1, source_target_pairs={{0,32},{1,33},{2,34},{3,35},{4,36},{5,37},{6,38},{7,39},{8,40},{9,... | collective-permute-start | bytes 294920 | tf_op jit(solution)/shard_map/ppermute | solution.py:60
  248.7 17.6 %collective-permute-start.78 = (f32[384,256]{1,0:T(8,128)S(1)}, f32[384,256]{1,0:T(8,128)S(1)}, u32[]{:S(2)}, u32[]{:S(2)}) collective-permute-start(f32[384,256]{1,0:T(8,128)S(1)} %pad_maximum_fusion.3.refs_2_), channel_id=1, source_target_pairs={{0,64},{1,9},{2,66},{3,11},{4,68},{5,13},{6,70},{7,15},{8,72},{9,1... | collective-permute-start | bytes 1179656 | tf_op jit(solution)/shard_map/ppermute | solution.py:60
  248.8 19.7 %collective-permute-start.79 = (f32[384,256]{1,0:T(8,128)S(1)}, f32[384,256]{1,0:T(8,128)S(1)}, u32[]{:S(2)}, u32[]{:S(2)}) collective-permute-start(f32[384,256]{1,0:T(8,128)S(1)} %pad_maximum_fusion.3.refs_2_), channel_id=1, source_target_pairs={{0,192},{1,25},{2,194},{3,27},{4,196},{5,29},{6,198},{7,31},{8,200... | collective-permute-start | bytes 1179656 | tf_op jit(solution)/shard_map/ppermute | solution.py:60
  251.4 17.0 %collective-permute-start.80 = (f32[384,256]{1,0:T(8,128)S(1)}, f32[384,256]{1,0:T(8,128)S(1)}, u32[]{:S(2)}, u32[]{:S(2)}) collective-permute-start(f32[384,256]{1,0:T(8,128)S(1)} %pad_maximum_fusion.3.refs_2_), channel_id=1, source_target_pairs={{0,128},{1,17},{2,130},{3,19},{4,132},{5,21},{6,134},{7,23},{8,136... | collective-permute-start | bytes 1179656 | tf_op jit(solution)/shard_map/ppermute | solution.py:60
  263.5 7.9 %collective-permute-start.73 = (f32[384,256]{1,0:T(8,128)S(1)}, f32[384,256]{1,0:T(8,128)S(1)}, u32[]{:S(2)}, u32[]{:S(2)}) collective-permute-start(f32[384,256]{1,0:T(8,128)S(1)} %constant_dynamic-update-slice_fusion.20.refs_3_), channel_id=1, source_target_pairs={{0,64},{1,9},{2,66},{3,11},{4,68},{5,13},{6,70},{7,15},{8,72},{9,1... | collective-permute-start | bytes 1179656 | tf_op jit(solution)/shard_map/ppermute | solution.py:60
  263.7 11.5 %collective-permute-start.74 = (f32[384,256]{1,0:T(8,128)S(1)}, f32[384,256]{1,0:T(8,128)S(1)}, u32[]{:S(2)}, u32[]{:S(2)}) collective-permute-start(f32[384,256]{1,0:T(8,128)S(1)} %constant_dynamic-update-slice_fusion.20.refs_3_), channel_id=1, source_target_pairs={{0,192},{1,25},{2,194},{3,27},{4,196},{5,29},{6,198},{7,31},{8,200... | collective-permute-start | bytes 1179656 | tf_op jit(solution)/shard_map/ppermute | solution.py:60
  266.3 10.8 %collective-permute-start.72 = (f32[384,256]{1,0:T(8,128)S(1)}, f32[384,256]{1,0:T(8,128)S(1)}, u32[]{:S(2)}, u32[]{:S(2)}) collective-permute-start(f32[384,256]{1,0:T(8,128)S(1)} %constant_dynamic-update-slice_fusion.20.refs_3_), channel_id=1, source_target_pairs={{0,128},{1,17},{2,130},{3,19},{4,132},{5,21},{6,134},{7,23},{8,136... | collective-permute-start | bytes 1179656 | tf_op jit(solution)/shard_map/ppermute | solution.py:60
  279.0 8.8 %collective-permute-start.81 = (f32[384,256]{1,0:T(8,128)S(1)}, f32[384,256]{1,0:T(8,128)S(1)}, u32[]{:S(2)}, u32[]{:S(2)}) collective-permute-start(f32[384,256]{1,0:T(8,128)S(1)} %get-tuple-element.23), channel_id=1, source_target_pairs={{0,1},{1,0},{2,3},{3,2},{4,5},{5,4},{6,7},{7,6},{8,9},{9,8},{10,11... | collective-permute-start | bytes 1179656 | tf_op jit(solution)/shard_map/ppermute | solution.py:60
  289.8 8.9 %collective-permute-start.83 = (f32[96,256]{1,0:T(8,128)S(1)}, f32[96,256]{1,0:T(8,128)S(1)}, u32[]{:S(2)}, u32[]{:S(2)}) collective-permute-start(f32[96,256]{1,0:T(8,128)S(1)} %get-tuple-element.32), channel_id=1, source_target_pairs={{0,4},{1,5},{2,6},{3,7},{4,0},{5,1},{6,2},{7,3},{8,12},{9,13},{10,... | collective-permute-start | bytes 294920 | tf_op jit(solution)/shard_map/ppermute | solution.py:60
  289.8 8.9 %collective-permute-start.84 = (f32[96,256]{1,0:T(8,128)S(1)}, f32[96,256]{1,0:T(8,128)S(1)}, u32[]{:S(2)}, u32[]{:S(2)}) collective-permute-start(f32[96,256]{1,0:T(8,128)S(1)} %get-tuple-element.31), channel_id=1, source_target_pairs={{0,6},{1,7},{2,0},{3,1},{4,2},{5,3},{6,4},{7,5},{8,14},{9,15},{10,... | collective-permute-start | bytes 294920 | tf_op jit(solution)/shard_map/ppermute | solution.py:60
  298.8 7.2 %collective-permute-start.93 = (f32[96,256]{1,0:T(8,128)S(1)}, f32[96,256]{1,0:T(8,128)S(1)}, u32[]{:S(2)}, u32[]{:S(2)}) collective-permute-start(f32[96,256]{1,0:T(8,128)S(1)} %fusion.8), channel_id=1, source_target_pairs={{0,16},{1,129},{2,18},{3,131},{4,20},{5,133},{6,22},{7,135},{8,24}... | collective-permute-start | bytes 294920 | tf_op jit(solution)/shard_map/ppermute | solution.py:60
  302.9 9.3 %collective-permute-start.85 = (f32[96,256]{1,0:T(8,128)S(1)}, f32[96,256]{1,0:T(8,128)S(1)}, u32[]{:S(2)}, u32[]{:S(2)}) collective-permute-start(f32[96,256]{1,0:T(8,128)S(1)} %fusion.8), channel_id=1, source_target_pairs={{0,32},{1,33},{2,34},{3,35},{4,36},{5,37},{6,38},{7,39},{8,40},{9,... | collective-permute-start | bytes 294920 | tf_op jit(solution)/shard_map/ppermute | solution.py:60
  306.7 17.7 %collective-permute-start.95 = (f32[384,256]{1,0:T(8,128)S(1)}, f32[384,256]{1,0:T(8,128)S(1)}, u32[]{:S(2)}, u32[]{:S(2)}) collective-permute-start(f32[384,256]{1,0:T(8,128)S(1)} %pad_maximum_fusion.4.refs_2_), channel_id=1, source_target_pairs={{0,64},{1,9},{2,66},{3,11},{4,68},{5,13},{6,70},{7,15},{8,72},{9,1... | collective-permute-start | bytes 1179656 | tf_op jit(solution)/shard_map/ppermute | solution.py:60
  306.8 19.8 %collective-permute-start.96 = (f32[384,256]{1,0:T(8,128)S(1)}, f32[384,256]{1,0:T(8,128)S(1)}, u32[]{:S(2)}, u32[]{:S(2)}) collective-permute-start(f32[384,256]{1,0:T(8,128)S(1)} %pad_maximum_fusion.4.refs_2_), channel_id=1, source_target_pairs={{0,192},{1,25},{2,194},{3,27},{4,196},{5,29},{6,198},{7,31},{8,200... | collective-permute-start | bytes 1179656 | tf_op jit(solution)/shard_map/ppermute | solution.py:60
  309.5 17.1 %collective-permute-start.97 = (f32[384,256]{1,0:T(8,128)S(1)}, f32[384,256]{1,0:T(8,128)S(1)}, u32[]{:S(2)}, u32[]{:S(2)}) collective-permute-start(f32[384,256]{1,0:T(8,128)S(1)} %pad_maximum_fusion.4.refs_2_), channel_id=1, source_target_pairs={{0,128},{1,17},{2,130},{3,19},{4,132},{5,21},{6,134},{7,23},{8,136... | collective-permute-start | bytes 1179656 | tf_op jit(solution)/shard_map/ppermute | solution.py:60
  321.7 7.9 %collective-permute-start.90 = (f32[384,256]{1,0:T(8,128)S(1)}, f32[384,256]{1,0:T(8,128)S(1)}, u32[]{:S(2)}, u32[]{:S(2)}) collective-permute-start(f32[384,256]{1,0:T(8,128)S(1)} %constant_dynamic-update-slice_fusion.24.refs_3_), channel_id=1, source_target_pairs={{0,64},{1,9},{2,66},{3,11},{4,68},{5,13},{6,70},{7,15},{8,72},{9,1... | collective-permute-start | bytes 1179656 | tf_op jit(solution)/shard_map/ppermute | solution.py:60
  322.9 7.3 %collective-permute-start.91 = (f32[384,256]{1,0:T(8,128)S(1)}, f32[384,256]{1,0:T(8,128)S(1)}, u32[]{:S(2)}, u32[]{:S(2)}) collective-permute-start(f32[384,256]{1,0:T(8,128)S(1)} %constant_dynamic-update-slice_fusion.24.refs_3_), channel_id=1, source_target_pairs={{0,192},{1,25},{2,194},{3,27},{4,196},{5,29},{6,198},{7,31},{8,200... | collective-permute-start | bytes 1179656 | tf_op jit(solution)/shard_map/ppermute | solution.py:60
  324.5 9.4 %collective-permute-start.89 = (f32[384,256]{1,0:T(8,128)S(1)}, f32[384,256]{1,0:T(8,128)S(1)}, u32[]{:S(2)}, u32[]{:S(2)}) collective-permute-start(f32[384,256]{1,0:T(8,128)S(1)} %constant_dynamic-update-slice_fusion.24.refs_3_), channel_id=1, source_target_pairs={{0,128},{1,17},{2,130},{3,19},{4,132},{5,21},{6,134},{7,23},{8,136... | collective-permute-start | bytes 1179656 | tf_op jit(solution)/shard_map/ppermute | solution.py:60
  335.9 9.5 %collective-permute-start.98 = (f32[384,256]{1,0:T(8,128)S(1)}, f32[384,256]{1,0:T(8,128)S(1)}, u32[]{:S(2)}, u32[]{:S(2)}) collective-permute-start(f32[384,256]{1,0:T(8,128)S(1)} %get-tuple-element.25), channel_id=1, source_target_pairs={{0,1},{1,0},{2,3},{3,2},{4,5},{5,4},{6,7},{7,6},{8,9},{9,8},{10,11... | collective-permute-start | bytes 1179656 | tf_op jit(solution)/shard_map/ppermute | solution.py:60
  349.7 7.0 %collective-permute-start.99 = (f32[96,256]{1,0:T(8,128)S(1)}, f32[96,256]{1,0:T(8,128)S(1)}, u32[]{:S(2)}, u32[]{:S(2)}) collective-permute-start(f32[96,256]{1,0:T(8,128)S(1)} %get-tuple-element.30), channel_id=1, source_target_pairs={{0,2},{1,3},{2,4},{3,5},{4,6},{5,7},{6,0},{7,1},{8,10},{9,11},{10,... | collective-permute-start | bytes 294920 | tf_op jit(solution)/shard_map/ppermute | solution.py:60
  (43 other events, 267.4 us)
where the time goes:
time: 404 us; the launch traced here: 398 us
  starting transfers between devices  158 us (39%)
  waiting for transfers between devices  145 us (36%)
  Pallas kernels  54 us (13%)
  blocking collectives  31.9 us (8%)
  local copies, waits for them, and re-layouts  5.09 us (1%)
    ppermute x104, starting transfers between devices, send(): return lax.ppermute(value, AX, moves)  158 us
    ppermute x104, waiting for transfers between devices, send(): return lax.ppermute(value, AX, moves)  145 us
    pallas_call x24, Pallas kernels, product(): pl.pallas_call(functools.partial(product_kernel, tuple(parts), acc is not...  47.9 us
    all_to_all x1, blocking collectives, on_device(): lax.all_to_all(half.reshape(16, 8, VECS), ('x', 'y'), 0, 0).sum(axis=0)  11.4 us
    all_to_all x1, blocking collectives, on_device(): lax.all_to_all(jnp.broadcast_to(piece, (8, 8, VECS)), ('zh', 'zl'), 0, 0)  10.3 us
    all_to_all x1, blocking collectives, on_device(): lax.all_to_all(jnp.broadcast_to(every, (16, 8, VECS)), ('x', 'y'), 0, 0)  10.2 us
  transfers between devices with their start and end apart: 104, of which 70 were waited for; matrix products, arithmetic and copies ran while one was open for 0% of the time, Pallas kernels for 11%

commit v1 on v0

v1 whole, which is shorter than its diff:
```python
import functools

import jax
import jax.numpy as jnp
from jax import lax
from jax.experimental import pallas as pl
from jax.experimental.pallas import tpu as pltpu
from jax.sharding import Mesh, PartitionSpec as P


ORDER = 24576
VECS = 256
DEGREE = 6
SH = 96
LOCAL = 768
COLS = 3072

filter_center = 2.75
filter_half = 1.75
filter_lower = 0.0


AX = ("x", "zh", "y", "zl", "core")
DIMS = (4, 2, 4, 4, 2)


def lin(x, zh, y, zl, core):
    return (((x * 2 + zh) * 4 + y) * 4 + zl) * 2 + core


def pairs(move):
    out = []
    for x in range(4):
        for zh in range(2):
            for y in range(4):
                for zl in range(4):
                    for core in range(2):
                        out.append((lin(x, zh, y, zl, core), lin(*move(x, zh, y, zl, core))))
    return out


SWAP_CORE = pairs(lambda x, zh, y, zl, core: (x, zh, y, zl, 1 - core))
SWAP_ZH = pairs(lambda x, zh, y, zl, core: (x, 1 - zh, y, zl, core))


def along_y(x, zh, y, zl, core, s):
    return (x, zh, (y + s) % 4, zl, core)


def along_x(x, zh, y, zl, core, s):
    return ((x + s) % 4, zh, y, zl, core)


FIRST = [pairs(lambda x, zh, y, zl, core, s=s: (along_x if core else along_y)(x, zh, y, zl, core, s)) for s in range(4)]
SECOND = [pairs(lambda x, zh, y, zl, core, s=s: (along_y if core else along_x)(x, zh, y, zl, core, s)) for s in range(4)]
ALONG_ZL = [pairs(lambda x, zh, y, zl, core, s=s: (x, zh, y, (zl + s) % 4, core)) for s in range(4)]


def send(value, moves):
    return lax.ppermute(value, AX, moves)


HALF = 4 * SH
BLOCKS = COLS // HALF


def position():
    x, zh, y, zl, core = (lax.axis_index(a) for a in AX)
    return core, zl, zh, jnp.where(core == 0, x, y), jnp.where(core == 0, y, x)


def split_kernel(h_ref, out_ref):
    core = position()[0]

    def write(order):
        h = h_ref[...]
        for block in range(BLOCKS):
            part = jnp.concatenate([h[:, i * SH : (i + 1) * SH] for i in order[4 * block : 4 * block + 4]], axis=1)
            hi = part.astype(jnp.bfloat16)
            out_ref[block, :, :HALF] = hi
            out_ref[block, :, HALF:] = (part - hi.astype(jnp.float32)).astype(jnp.bfloat16)

    @pl.when(core == 0)
    def _():
        write(list(range(32)))

    @pl.when(core != 0)
    def _():
        write([(x * 2 + zh) * 4 + y for y in range(4) for zh in range(2) for x in range(4)])


def split_operator(coupling):
    return pl.pallas_call(
        split_kernel,
        grid=(LOCAL // 96,),
        in_specs=[pl.BlockSpec((96, COLS), lambda i: (i, 0))],
        out_specs=pl.BlockSpec((BLOCKS, 96, 2 * HALF), lambda i: (0, i, 0)),
        out_shape=jax.ShapeDtypeStruct((BLOCKS, LOCAL, 2 * HALF), jnp.bfloat16),
        compiler_params=pltpu.CompilerParams(vmem_limit_bytes=16 << 20),
    )(coupling)


def product_kernel(blocks, fetch, has_acc, last, *refs):
    operator, refs = refs[0], refs[1:]
    n = sum(count for _, _, count in blocks)
    parts, refs = refs[:n], refs[n:]
    acc_in, refs = (refs[0], refs[1:]) if has_acc else (None, refs)
    outs, refs = (refs[:2], refs[2:]) if last else (refs[:1], refs[1:])
    core, zl, zh, own_u, own_v = position()

    def block_of(t, z):
        return ((own_u - t + 4) % 4) * 2 + (zh + z) % 2

    copies = []
    if fetch:
        whole, refs = refs[0], refs[1:]
        sems = refs[1]
        for k in range(BLOCKS):
            block = block_of(k // 2, k % 2)
            copies.append(pltpu.make_async_copy(operator.at[block], whole.at[block], sems.at[k]))
            copies[-1].start()
        operator = whole
    rows_of = refs[0]

    pieces = iter(parts)
    for b, (_, _, count) in enumerate(blocks):
        for s in range(4):
            if s % (4 // count) == 0:
                part = next(pieces)
            first = s % (4 // count) * SH
            rows = part[first : first + SH, :]
            hi = rows.astype(jnp.bfloat16)
            lo = (rows - hi.astype(jnp.float32)).astype(jnp.bfloat16)
            at = pl.multiple_of(((own_v - s + 4) % 4) * SH, SH)
            rows_of[b, pl.ds(at, SH), :] = lo
            rows_of[b, pl.ds(HALF + at, SH), :] = hi
    for copy in copies[: len(blocks)]:
        copy.wait()
    for half in range(2):
        m = slice(half * LOCAL // 2, (half + 1) * LOCAL // 2)
        acc = acc_in[m, :] if has_acc else None
        for b, (t, z, _) in enumerate(blocks):
            block = block_of(t, z)
            term = jnp.dot(operator[block, m, :], rows_of[b], preferred_element_type=jnp.float32)
            term += jnp.dot(operator[block, m, :HALF], rows_of[b, HALF:, :], preferred_element_type=jnp.float32)
            acc = term if acc is None else acc + term
        if not last:
            outs[0][m, :] = acc
            continue
        keep, give = outs
        for pair in range(2):
            to = pl.multiple_of(((half * 2 + pair - zl + 4) % 4) * SH, SH)
            even, odd = acc[pair * 2 * SH : pair * 2 * SH + SH], acc[pair * 2 * SH + SH : (pair + 1) * 2 * SH]

            @pl.when(core == 0)
            def _():
                keep[pl.ds(to, SH), :] = even
                give[pl.ds(to, SH), :] = odd

            @pl.when(core != 0)
            def _():
                keep[pl.ds(to, SH), :] = odd
                give[pl.ds(to, SH), :] = even

    for copy in copies[len(blocks) :]:
        copy.wait()


def product(operator, blocks, acc, fetch=False, last=False):
    vmem = pl.BlockSpec(memory_space=pltpu.VMEM)
    given = [a for _, _, arrays in blocks for a in arrays] + ([] if acc is None else [acc])
    out = [jax.ShapeDtypeStruct((HALF, VECS), jnp.float32)] * 2 if last else [jax.ShapeDtypeStruct((LOCAL, VECS), jnp.float32)]
    scratch = [pltpu.VMEM((len(blocks), 2 * HALF, VECS), jnp.bfloat16)]
    if fetch:
        out = out + [jax.ShapeDtypeStruct(operator.shape, operator.dtype)]
        scratch = scratch + [pltpu.SemaphoreType.DMA((BLOCKS,))]
    return pl.pallas_call(
        functools.partial(product_kernel, tuple((t, z, len(arrays)) for t, z, arrays in blocks), fetch, acc is not None, last),
        in_specs=[pl.BlockSpec(memory_space=pl.ANY) if fetch else vmem] + [vmem] * len(given),
        out_specs=[vmem] * len(out),
        out_shape=out,
        scratch_shapes=scratch,
        compiler_params=pltpu.CompilerParams(vmem_limit_bytes=20 << 20),
    )(operator, *given)


def on_device(coupling, vectors):
    core = lax.axis_index("core")
    operator = split_operator(coupling)

    def along_first(rows):
        near = {s: send(rows, FIRST[s]) for s in (2, 1, 3)}
        return jnp.concatenate([rows, near[1], near[2], near[3]], axis=0)

    def beside(rows):
        return send(rows, SECOND[1]), send(rows, SECOND[3])

    def opposite(low, high):
        return send(low[: 2 * SH], SECOND[1]), send(high[2 * SH :], SECOND[3])

    def apply(current):
        partner = send(current, SWAP_ZH)
        a = along_first(current)
        b = along_first(partner)
        a1, a3 = beside(a)
        b1, b3 = beside(b)
        acc, fast = product(operator, [(0, 0, [a]), (0, 1, [b])], None, fetch=True)
        acc, a1, a3 = lax.optimization_barrier((acc, a1, a3))
        a2 = opposite(a1, a3)
        (acc,) = product(fast, [(1, 0, [a1]), (3, 0, [a3])], acc)
        acc, b1, b3 = lax.optimization_barrier((acc, b1, b3))
        b2 = opposite(b1, b3)
        (acc,) = product(fast, [(1, 1, [b1]), (3, 1, [b3]), (2, 0, a2)], acc)
        keep, give = product(fast, [(2, 1, b2)], acc, last=True)
        total = keep + send(give, SWAP_CORE)
        here = {s: send(total[s * SH : (s + 1) * SH], ALONG_ZL[s]) for s in (2, 1, 3)}
        return (total[:SH] + here[1]) + (here[2] + here[3])

    def step(_, carry):
        _, previous, current = carry
        applied = apply(current)
        following = (2.0 / filter_half) * (applied - filter_center * current) - previous
        return previous, current, following

    at_lower = (filter_lower - filter_center) / filter_half
    before, scale = 1.0, at_lower
    for _ in range(DEGREE - 1):
        before, scale = scale, 2.0 * at_lower * scale - before
    zero = jnp.zeros_like(vectors)
    older, _, current = lax.fori_loop(0, DEGREE, step, (zero, zero, vectors))
    current = (0.5 / scale) * (current - older)

    local = jnp.dot(current.T, current, precision=lax.Precision.HIGHEST, preferred_element_type=jnp.float32)
    halves = local.reshape(2, 128, VECS)
    mine = lax.dynamic_index_in_dim(halves, core, 0, keepdims=False)
    other = lax.dynamic_index_in_dim(halves, 1 - core, 0, keepdims=False)
    half = mine + send(other, SWAP_CORE)
    piece = lax.all_to_all(half.reshape(16, 8, VECS), ("x", "y"), 0, 0).sum(axis=0)
    every = lax.all_to_all(jnp.broadcast_to(piece, (8, 8, VECS)), ("zh", "zl"), 0, 0).sum(axis=0) / ORDER
    half = lax.all_to_all(jnp.broadcast_to(every, (16, 8, VECS)), ("x", "y"), 0, 0).reshape(128, VECS)
    other = send(half, SWAP_CORE)
    gram = jnp.concatenate([jnp.where(core == 0, half, other), jnp.where(core == 0, other, half)], axis=0)
    return current, gram


def solution(mesh):
    fine = Mesh(mesh.devices.reshape(DIMS), AX)
    return jax.shard_map(
        on_device,
        mesh=fine,
        in_specs=(P(("x", "zh", "y"), ("zl", "core")), P(AX, None)),
        out_specs=(P(AX, None), P()),
        check_vma=False,
    )
```

time: 404 us -> 392 us (0.970)
  the two profiles are of different devices: /device:TPU:1 before, /device:TPU:2 now
where the time goes in v1:
time: 392 us; the launch traced here: 390 us
  starting transfers between devices  168 us (43%)
  waiting for transfers between devices  112 us (29%)
  Pallas kernels  55.4 us (14%)
  blocking collectives  41.5 us (11%)
  local copies, waits for them, and re-layouts  8.51 us (2%)
    ppermute x116, starting transfers between devices, send(): return lax.ppermute(value, AX, moves)  168 us
    ppermute x116, waiting for transfers between devices, send(): return lax.ppermute(value, AX, moves)  112 us
    pallas_call x24, Pallas kernels, product(): pl.pallas_call(functools.partial(product_kernel, tuple(((t, z, len(arrays...  50.2 us
    all_to_all x1, blocking collectives, on_device(): lax.all_to_all(jnp.broadcast_to(piece, (8, 8, VECS)), ('zh', 'zl'), 0, 0)  15.9 us
    all_to_all x1, blocking collectives, on_device(): lax.all_to_all(half.reshape(16, 8, VECS), ('x', 'y'), 0, 0).sum(axis=0)  14.3 us
    all_to_all x1, blocking collectives, on_device(): lax.all_to_all(jnp.broadcast_to(every, (16, 8, VECS)), ('x', 'y'), 0, 0)  11.2 us
  transfers between devices with their start and end apart: 116, of which 79 were waited for; matrix products, arithmetic and copies ran while one was open for 1% of the time, Pallas kernels for 11%

profile of v1, /device:TPU:2, one launch (start us, length us, event | category | flops | bytes accessed | tf_op | source)
XLA Modules:
  0.0 390.0 jit_solution(11465187568773794687)
XLA Ops:
  0.7 3.7 copy-done
  4.3 5.2 %shard_map.41 = bf16[8,768,768]{2,1,0:T(8,128)(2,1)} custom-call(f32[768,3072]{1,0:T(8,128)S(1)} %copy-done), custom_call_target="tpu_custom_call" | custom-call | tf_op jit(solution)/shard_map/pallas_call | solution.py:93
  9.6 333.9 %while.14 = (s32[]{:T(128)}, f32[96,256]{1,0:T(8,128)}, f32[96,256]{1,0:T(8,128)S(1)}, f32[96,256]{1,0:T(8,128)S(1)}, bf16[8,768,768]{2,1,0:T(8,128)(2,1)}, /*index=5*/s32[]{:T(128)}) while((s32[]{:T(128)}, f32[96,256]{1,0:T(8,128)}, f32[96,256]{1,0:T(8,128)S(1)}, f32[96,256]{1,0:T(8,128)S(1)}, bf16[8,768,768]{2,1,0:T(8,128)(2,1)}, ...), condition=%wide.region_1.0_spmd, body=%wide.region_0.0_spmd.sunk | while | flops 270338 | bytes 21136188 | solution.py:230
  9.6 7.3 %collective-permute-start.3 = (f32[96,256]{1,0:T(8,128)S(1)}, f32[96,256]{1,0:T(8,128)S(1)}, u32[]{:S(2)}, u32[]{:S(2)}) collective-permute-start(f32[96,256]{1,0:T(8,128)S(1)} %copy.17), channel_id=1, source_target_pairs={{0,32},{1,33},{2,34},{3,35},{4,36},{5,37},{6,38},{7,39},{8,40},{9,... | collective-permute-start | bytes 294920 | tf_op jit(solution)/shard_map/while/body/eval_jaxpr/ppermute | solution.py:60
  18.4 2.9 collective-permute-start.1
  22.7 2.3 collective-permute-done.1
  28.7 3.4 collective-permute-start.5
  34.1 2.2 collective-permute-done.5
  38.8 3.8 eval_jaxpr.4
  46.3 2.0 collective-permute-start.11
  60.0 1.9 collective-permute-start.18
  62.5 2.5 collective-permute-done.16
  65.1 3.4 collective-permute-done.17
  69.4 2.9 collective-permute-start.1
  76.9 2.1 collective-permute-start.7
  80.1 3.0 collective-permute-start.5
  83.4 2.2 collective-permute-done.4
  87.8 3.4 collective-permute-start.10
  91.2 3.8 eval_jaxpr.4
  99.0 2.3 collective-permute-start.11
  110.3 2.5 collective-permute-start.16
  115.9 2.1 collective-permute-done.16
  118.0 3.4 collective-permute-done.17
  121.4 5.6 %collective-permute-start.3 = (f32[96,256]{1,0:T(8,128)S(1)}, f32[96,256]{1,0:T(8,128)S(1)}, u32[]{:S(2)}, u32[]{:S(2)}) collective-permute-start(f32[96,256]{1,0:T(8,128)S(1)} %copy.17), channel_id=1, source_target_pairs={{0,32},{1,33},{2,34},{3,35},{4,36},{5,37},{6,38},{7,39},{8,40},{9,... | collective-permute-start | bytes 294920 | tf_op jit(solution)/shard_map/while/body/eval_jaxpr/ppermute | solution.py:60
  127.2 3.2 collective-permute-start.1
  135.0 2.1 collective-permute-start.7
  138.1 3.2 collective-permute-start.5
  141.4 2.5 collective-permute-done.4
  145.9 3.4 collective-permute-start.10
  149.3 3.8 eval_jaxpr.4
  157.1 2.3 collective-permute-start.11
  168.4 2.7 collective-permute-start.16
  176.0 3.4 collective-permute-done.17
  180.1 3.2 collective-permute-start.1
  187.9 2.1 collective-permute-start.7
  191.0 3.2 collective-permute-start.5
  194.3 2.5 collective-permute-done.4
  198.8 3.4 collective-permute-start.10
  202.2 3.8 eval_jaxpr.4
  210.0 2.3 collective-permute-start.11
  221.3 2.6 collective-permute-start.16
  229.0 3.4 collective-permute-done.17
  232.5 5.7 %collective-permute-start.3 = (f32[96,256]{1,0:T(8,128)S(1)}, f32[96,256]{1,0:T(8,128)S(1)}, u32[]{:S(2)}, u32[]{:S(2)}) collective-permute-start(f32[96,256]{1,0:T(8,128)S(1)} %copy.17), channel_id=1, source_target_pairs={{0,32},{1,33},{2,34},{3,35},{4,36},{5,37},{6,38},{7,39},{8,40},{9,... | collective-permute-start | bytes 294920 | tf_op jit(solution)/shard_map/while/body/eval_jaxpr/ppermute | solution.py:60
  238.3 3.2 collective-permute-start.1
  246.1 2.1 collective-permute-start.7
  249.1 3.2 collective-permute-start.5
  252.5 2.5 collective-permute-done.4
  256.9 3.4 collective-permute-start.10
  260.3 3.8 eval_jaxpr.4
  268.1 2.3 collective-permute-start.11
  279.4 2.6 collective-permute-start.16
  287.1 3.4 collective-permute-done.17
  291.3 3.2 collective-permute-start.1
  299.1 2.1 collective-permute-start.7
  302.0 3.2 collective-permute-start.5
  305.6 2.3 collective-permute-done.4
  309.8 3.4 collective-permute-start.10
  313.2 3.8 eval_jaxpr.4
  321.0 2.3 collective-permute-start.11
  332.4 2.6 collective-permute-start.16
  340.0 3.4 collective-permute-done.17
  346.3 14.3 %all_to_all.15 = f32[16,8,256]{2,1,0:T(8,128)S(1)} all-to-all(f32[16,8,256]{2,1,0:T(8,128)S(1)} %fusion.4), channel_id=1, replica_groups=mesh['x'=4,'zh'=2,'y'=4,'zl'=4,'core'=2] {'x','y'}, dimensions={0} | all-to-all | bytes 262144 | tf_op jit(solution)/shard_map/all_to_all | solution.py:238
  360.7 15.9 %all_to_all.16 = f32[8,8,256]{2,1,0:T(8,128)S(1)} all-to-all(f32[8,8,256]{2,1,0:T(8,128)S(1)} %broadcast_in_dim.10), channel_id=1, replica_groups=mesh['x'=4,'zh'=2,'y'=4,'zl'=4,'core'=2] {'zh','zl'}, dimensions={0} | all-to-all | bytes 131072 | tf_op jit(solution)/shard_map/all_to_all | solution.py:239
  376.7 11.2 %all_to_all.17 = f32[16,8,256]{2,1,0:T(8,128)S(1)} all-to-all(f32[16,8,256]{2,1,0:T(8,128)S(1)} %broadcast_in_dim.11), channel_id=1, replica_groups=mesh['x'=4,'zh'=2,'y'=4,'zl'=4,'core'=2] {'x','y'}, dimensions={0} | all-to-all | bytes 262144 | tf_op jit(solution)/shard_map/all_to_all | solution.py:240
  (324 shorter events, 161.6 us)
Async XLA Ops:
  9.6 18.5 %collective-permute-start.3 = (f32[96,256]{1,0:T(8,128)S(1)}, f32[96,256]{1,0:T(8,128)S(1)}, u32[]{:S(2)}, u32[]{:S(2)}) collective-permute-start(f32[96,256]{1,0:T(8,128)S(1)} %copy.17), channel_id=1, source_target_pairs={{0,32},{1,33},{2,34},{3,35},{4,36},{5,37},{6,38},{7,39},{8,40},{9,... | collective-permute-start | bytes 294920 | tf_op jit(solution)/shard_map/while/body/eval_jaxpr/ppermute | solution.py:60
  26.0 16.7 %collective-permute-start.7 = (f32[384,256]{1,0:T(8,128)S(1)}, f32[384,256]{1,0:T(8,128)S(1)}, u32[]{:S(2)}, u32[]{:S(2)}) collective-permute-start(f32[384,256]{1,0:T(8,128)S(1)} %constant_dynamic-update-slice_fusion.19.refs_1_), channel_id=1, source_target_pairs={{0,64},{1,9},{2,66},{3,11},{4,68},{5,13},{6,70},{7,15},{8,72},{9,1... | collective-permute-start | bytes 1179656 | tf_op jit(solution)/shard_map/while/body/eval_jaxpr/ppermute | solution.py:60
  27.5 15.2 %collective-permute-start.8 = (f32[384,256]{1,0:T(8,128)S(1)}, f32[384,256]{1,0:T(8,128)S(1)}, u32[]{:S(2)}, u32[]{:S(2)}) collective-permute-start(f32[384,256]{1,0:T(8,128)S(1)} %constant_dynamic-update-slice_fusion.19.refs_1_), channel_id=1, source_target_pairs={{0,192},{1,25},{2,194},{3,27},{4,196},{5,29},{6,198},{7,31},{8,200... | collective-permute-start | bytes 1179656 | tf_op jit(solution)/shard_map/while/body/eval_jaxpr/ppermute | solution.py:60
  28.7 7.6 %collective-permute-start.5 = (f32[96,256]{1,0:T(8,128)S(1)}, f32[96,256]{1,0:T(8,128)S(1)}, u32[]{:S(2)}, u32[]{:S(2)}) collective-permute-start(f32[96,256]{1,0:T(8,128)S(1)} %collective-permute-done.3), channel_id=1, source_target_pairs={{0,16},{1,129},{2,18},{3,131},{4,20},{5,133},{6,22},{7,135},{8,24}... | collective-permute-start | bytes 294920 | tf_op jit(solution)/shard_map/while/body/eval_jaxpr/ppermute | solution.py:60
  36.7 9.5 %collective-permute-start.10 = (f32[384,256]{1,0:T(8,128)S(1)}, f32[384,256]{1,0:T(8,128)S(1)}, u32[]{:S(2)}, u32[]{:S(2)}) collective-permute-start(f32[384,256]{1,0:T(8,128)S(1)} %constant_dynamic-update-slice_fusion.23.refs_2_), channel_id=1, source_target_pairs={{0,192},{1,25},{2,194},{3,27},{4,196},{5,29},{6,198},{7,31},{8,200... | collective-permute-start | bytes 1179656 | tf_op jit(solution)/shard_map/while/body/eval_jaxpr/ppermute | solution.py:60
  38.5 7.8 %collective-permute-start.9 = (f32[384,256]{1,0:T(8,128)S(1)}, f32[384,256]{1,0:T(8,128)S(1)}, u32[]{:S(2)}, u32[]{:S(2)}) collective-permute-start(f32[384,256]{1,0:T(8,128)S(1)} %constant_dynamic-update-slice_fusion.23.refs_2_), channel_id=1, source_target_pairs={{0,64},{1,9},{2,66},{3,11},{4,68},{5,13},{6,70},{7,15},{8,72},{9,1... | collective-permute-start | bytes 1179656 | tf_op jit(solution)/shard_map/while/body/eval_jaxpr/ppermute | solution.py:60
  57.4 7.6 %collective-permute-start.16 = (f32[96,256]{1,0:T(8,128)S(1)}, f32[96,256]{1,0:T(8,128)S(1)}, u32[]{:S(2)}, u32[]{:S(2)}) collective-permute-start(f32[96,256]{1,0:T(8,128)S(1)} %get-tuple-element.108), channel_id=1, source_target_pairs={{0,2},{1,3},{2,4},{3,5},{4,6},{5,7},{6,0},{7,1},{8,10},{9,11},{10,... | collective-permute-start | bytes 294920 | tf_op jit(solution)/shard_map/while/body/eval_jaxpr/ppermute | solution.py:60
  58.5 9.9 %collective-permute-start.17 = (f32[96,256]{1,0:T(8,128)S(1)}, f32[96,256]{1,0:T(8,128)S(1)}, u32[]{:S(2)}, u32[]{:S(2)}) collective-permute-start(f32[96,256]{1,0:T(8,128)S(1)} %get-tuple-element.109), channel_id=1, source_target_pairs={{0,4},{1,5},{2,6},{3,7},{4,0},{5,1},{6,2},{7,3},{8,12},{9,13},{10,... | collective-permute-start | bytes 294920 | tf_op jit(solution)/shard_map/while/body/eval_jaxpr/ppermute | solution.py:60
  60.0 8.5 %collective-permute-start.18 = (f32[96,256]{1,0:T(8,128)S(1)}, f32[96,256]{1,0:T(8,128)S(1)}, u32[]{:S(2)}, u32[]{:S(2)}) collective-permute-start(f32[96,256]{1,0:T(8,128)S(1)} %get-tuple-element.110), channel_id=1, source_target_pairs={{0,6},{1,7},{2,0},{3,1},{4,2},{5,3},{6,4},{7,5},{8,14},{9,15},{10,... | collective-permute-start | bytes 294920 | tf_op jit(solution)/shard_map/while/body/eval_jaxpr/ppermute | solution.py:60
  68.5 10.6 %collective-permute-start.3 = (f32[96,256]{1,0:T(8,128)S(1)}, f32[96,256]{1,0:T(8,128)S(1)}, u32[]{:S(2)}, u32[]{:S(2)}) collective-permute-start(f32[96,256]{1,0:T(8,128)S(1)} %copy.17), channel_id=1, source_target_pairs={{0,32},{1,33},{2,34},{3,35},{4,36},{5,37},{6,38},{7,39},{8,40},{9,... | collective-permute-start | bytes 294920 | tf_op jit(solution)/shard_map/while/body/eval_jaxpr/ppermute | solution.py:60
  76.9 18.1 %collective-permute-start.7 = (f32[384,256]{1,0:T(8,128)S(1)}, f32[384,256]{1,0:T(8,128)S(1)}, u32[]{:S(2)}, u32[]{:S(2)}) collective-permute-start(f32[384,256]{1,0:T(8,128)S(1)} %constant_dynamic-update-slice_fusion.19.refs_1_), channel_id=1, source_target_pairs={{0,64},{1,9},{2,66},{3,11},{4,68},{5,13},{6,70},{7,15},{8,72},{9,1... | collective-permute-start | bytes 1179656 | tf_op jit(solution)/shard_map/while/body/eval_jaxpr/ppermute | solution.py:60
  79.0 16.0 %collective-permute-start.8 = (f32[384,256]{1,0:T(8,128)S(1)}, f32[384,256]{1,0:T(8,128)S(1)}, u32[]{:S(2)}, u32[]{:S(2)}) collective-permute-start(f32[384,256]{1,0:T(8,128)S(1)} %constant_dynamic-update-slice_fusion.19.refs_1_), channel_id=1, source_target_pairs={{0,192},{1,25},{2,194},{3,27},{4,196},{5,29},{6,198},{7,31},{8,200... | collective-permute-start | bytes 1179656 | tf_op jit(solution)/shard_map/while/body/eval_jaxpr/ppermute | solution.py:60
  87.8 10.8 %collective-permute-start.10 = (f32[384,256]{1,0:T(8,128)S(1)}, f32[384,256]{1,0:T(8,128)S(1)}, u32[]{:S(2)}, u32[]{:S(2)}) collective-permute-start(f32[384,256]{1,0:T(8,128)S(1)} %constant_dynamic-update-slice_fusion.23.refs_2_), channel_id=1, source_target_pairs={{0,192},{1,25},{2,194},{3,27},{4,196},{5,29},{6,198},{7,31},{8,200... | collective-permute-start | bytes 1179656 | tf_op jit(solution)/shard_map/while/body/eval_jaxpr/ppermute | solution.py:60
  91.2 7.8 %collective-permute-start.9 = (f32[384,256]{1,0:T(8,128)S(1)}, f32[384,256]{1,0:T(8,128)S(1)}, u32[]{:S(2)}, u32[]{:S(2)}) collective-permute-start(f32[384,256]{1,0:T(8,128)S(1)} %constant_dynamic-update-slice_fusion.23.refs_2_), channel_id=1, source_target_pairs={{0,64},{1,9},{2,66},{3,11},{4,68},{5,13},{6,70},{7,15},{8,72},{9,1... | collective-permute-start | bytes 1179656 | tf_op jit(solution)/shard_map/while/body/eval_jaxpr/ppermute | solution.py:60
  95.1 7.2 %collective-permute-start.13 = (f32[192,256]{1,0:T(8,128)S(1)}, f32[192,256]{1,0:T(8,128)S(1)}, u32[]{:S(2)}, u32[]{:S(2)}) collective-permute-start(f32[192,256]{1,0:T(8,128)S(1)} %slice.54), channel_id=1, source_target_pairs={{0,64},{1,9},{2,66},{3,11},{4,68},{5,13},{6,70},{7,15},{8,72},{9,1... | collective-permute-start | bytes 589832 | tf_op jit(solution)/shard_map/while/body/eval_jaxpr/ppermute | solution.py:60
  96.6 6.9 %collective-permute-start.14 = (f32[192,256]{1,0:T(8,128)S(1)}, f32[192,256]{1,0:T(8,128)S(1)}, u32[]{:S(2)}, u32[]{:S(2)}) collective-permute-start(f32[192,256]{1,0:T(8,128)S(1)} %slice.55), channel_id=1, source_target_pairs={{0,192},{1,25},{2,194},{3,27},{4,196},{5,29},{6,198},{7,31},{8,200... | collective-permute-start | bytes 589832 | tf_op jit(solution)/shard_map/while/body/eval_jaxpr/ppermute | solution.py:60
  99.0 6.9 %collective-permute-start.11 = (f32[192,256]{1,0:T(8,128)S(1)}, f32[192,256]{1,0:T(8,128)S(1)}, u32[]{:S(2)}, u32[]{:S(2)}) collective-permute-start(f32[192,256]{1,0:T(8,128)S(1)} %slice.52), channel_id=1, source_target_pairs={{0,64},{1,9},{2,66},{3,11},{4,68},{5,13},{6,70},{7,15},{8,72},{9,1... | collective-permute-start | bytes 589832 | tf_op jit(solution)/shard_map/while/body/eval_jaxpr/ppermute | solution.py:60
  110.3 7.6 %collective-permute-start.16 = (f32[96,256]{1,0:T(8,128)S(1)}, f32[96,256]{1,0:T(8,128)S(1)}, u32[]{:S(2)}, u32[]{:S(2)}) collective-permute-start(f32[96,256]{1,0:T(8,128)S(1)} %get-tuple-element.108), channel_id=1, source_target_pairs={{0,2},{1,3},{2,4},{3,5},{4,6},{5,7},{6,0},{7,1},{8,10},{9,11},{10,... | collective-permute-start | bytes 294920 | tf_op jit(solution)/shard_map/while/body/eval_jaxpr/ppermute | solution.py:60
  112.8 8.5 %collective-permute-start.17 = (f32[96,256]{1,0:T(8,128)S(1)}, f32[96,256]{1,0:T(8,128)S(1)}, u32[]{:S(2)}, u32[]{:S(2)}) collective-permute-start(f32[96,256]{1,0:T(8,128)S(1)} %get-tuple-element.109), channel_id=1, source_target_pairs={{0,4},{1,5},{2,6},{3,7},{4,0},{5,1},{6,2},{7,3},{8,12},{9,13},{10,... | collective-permute-start | bytes 294920 | tf_op jit(solution)/shard_map/while/body/eval_jaxpr/ppermute | solution.py:60
  113.7 7.6 %collective-permute-start.18 = (f32[96,256]{1,0:T(8,128)S(1)}, f32[96,256]{1,0:T(8,128)S(1)}, u32[]{:S(2)}, u32[]{:S(2)}) collective-permute-start(f32[96,256]{1,0:T(8,128)S(1)} %get-tuple-element.110), channel_id=1, source_target_pairs={{0,6},{1,7},{2,0},{3,1},{4,2},{5,3},{6,4},{7,5},{8,14},{9,15},{10,... | collective-permute-start | bytes 294920 | tf_op jit(solution)/shard_map/while/body/eval_jaxpr/ppermute | solution.py:60
  121.4 15.8 %collective-permute-start.3 = (f32[96,256]{1,0:T(8,128)S(1)}, f32[96,256]{1,0:T(8,128)S(1)}, u32[]{:S(2)}, u32[]{:S(2)}) collective-permute-start(f32[96,256]{1,0:T(8,128)S(1)} %copy.17), channel_id=1, source_target_pairs={{0,32},{1,33},{2,34},{3,35},{4,36},{5,37},{6,38},{7,39},{8,40},{9,... | collective-permute-start | bytes 294920 | tf_op jit(solution)/shard_map/while/body/eval_jaxpr/ppermute | solution.py:60
  135.0 18.1 %collective-permute-start.7 = (f32[384,256]{1,0:T(8,128)S(1)}, f32[384,256]{1,0:T(8,128)S(1)}, u32[]{:S(2)}, u32[]{:S(2)}) collective-permute-start(f32[384,256]{1,0:T(8,128)S(1)} %constant_dynamic-update-slice_fusion.19.refs_1_), channel_id=1, source_target_pairs={{0,64},{1,9},{2,66},{3,11},{4,68},{5,13},{6,70},{7,15},{8,72},{9,1... | collective-permute-start | bytes 1179656 | tf_op jit(solution)/shard_map/while/body/eval_jaxpr/ppermute | solution.py:60
  137.1 16.0 %collective-permute-start.8 = (f32[384,256]{1,0:T(8,128)S(1)}, f32[384,256]{1,0:T(8,128)S(1)}, u32[]{:S(2)}, u32[]{:S(2)}) collective-permute-start(f32[384,256]{1,0:T(8,128)S(1)} %constant_dynamic-update-slice_fusion.19.refs_1_), channel_id=1, source_target_pairs={{0,192},{1,25},{2,194},{3,27},{4,196},{5,29},{6,198},{7,31},{8,200... | collective-permute-start | bytes 1179656 | tf_op jit(solution)/shard_map/while/body/eval_jaxpr/ppermute | solution.py:60
  138.1 7.0 %collective-permute-start.5 = (f32[96,256]{1,0:T(8,128)S(1)}, f32[96,256]{1,0:T(8,128)S(1)}, u32[]{:S(2)}, u32[]{:S(2)}) collective-permute-start(f32[96,256]{1,0:T(8,128)S(1)} %collective-permute-done.3), channel_id=1, source_target_pairs={{0,16},{1,129},{2,18},{3,131},{4,20},{5,133},{6,22},{7,135},{8,24}... | collective-permute-start | bytes 294920 | tf_op jit(solution)/shard_map/while/body/eval_jaxpr/ppermute | solution.py:60
  145.9 10.8 %collective-permute-start.10 = (f32[384,256]{1,0:T(8,128)S(1)}, f32[384,256]{1,0:T(8,128)S(1)}, u32[]{:S(2)}, u32[]{:S(2)}) collective-permute-start(f32[384,256]{1,0:T(8,128)S(1)} %constant_dynamic-update-slice_fusion.23.refs_2_), channel_id=1, source_target_pairs={{0,192},{1,25},{2,194},{3,27},{4,196},{5,29},{6,198},{7,31},{8,200... | collective-permute-start | bytes 1179656 | tf_op jit(solution)/shard_map/while/body/eval_jaxpr/ppermute | solution.py:60
  149.3 7.8 %collective-permute-start.9 = (f32[384,256]{1,0:T(8,128)S(1)}, f32[384,256]{1,0:T(8,128)S(1)}, u32[]{:S(2)}, u32[]{:S(2)}) collective-permute-start(f32[384,256]{1,0:T(8,128)S(1)} %constant_dynamic-update-slice_fusion.23.refs_2_), channel_id=1, source_target_pairs={{0,64},{1,9},{2,66},{3,11},{4,68},{5,13},{6,70},{7,15},{8,72},{9,1... | collective-permute-start | bytes 1179656 | tf_op jit(solution)/shard_map/while/body/eval_jaxpr/ppermute | solution.py:60
  153.2 7.2 %collective-permute-start.13 = (f32[192,256]{1,0:T(8,128)S(1)}, f32[192,256]{1,0:T(8,128)S(1)}, u32[]{:S(2)}, u32[]{:S(2)}) collective-permute-start(f32[192,256]{1,0:T(8,128)S(1)} %slice.54), channel_id=1, source_target_pairs={{0,64},{1,9},{2,66},{3,11},{4,68},{5,13},{6,70},{7,15},{8,72},{9,1... | collective-permute-start | bytes 589832 | tf_op jit(solution)/shard_map/while/body/eval_jaxpr/ppermute | solution.py:60
  154.7 6.9 %collective-permute-start.14 = (f32[192,256]{1,0:T(8,128)S(1)}, f32[192,256]{1,0:T(8,128)S(1)}, u32[]{:S(2)}, u32[]{:S(2)}) collective-permute-start(f32[192,256]{1,0:T(8,128)S(1)} %slice.55), channel_id=1, source_target_pairs={{0,192},{1,25},{2,194},{3,27},{4,196},{5,29},{6,198},{7,31},{8,200... | collective-permute-start | bytes 589832 | tf_op jit(solution)/shard_map/while/body/eval_jaxpr/ppermute | solution.py:60
  157.1 6.9 %collective-permute-start.11 = (f32[192,256]{1,0:T(8,128)S(1)}, f32[192,256]{1,0:T(8,128)S(1)}, u32[]{:S(2)}, u32[]{:S(2)}) collective-permute-start(f32[192,256]{1,0:T(8,128)S(1)} %slice.52), channel_id=1, source_target_pairs={{0,64},{1,9},{2,66},{3,11},{4,68},{5,13},{6,70},{7,15},{8,72},{9,1... | collective-permute-start | bytes 589832 | tf_op jit(solution)/shard_map/while/body/eval_jaxpr/ppermute | solution.py:60
  168.4 7.6 %collective-permute-start.16 = (f32[96,256]{1,0:T(8,128)S(1)}, f32[96,256]{1,0:T(8,128)S(1)}, u32[]{:S(2)}, u32[]{:S(2)}) collective-permute-start(f32[96,256]{1,0:T(8,128)S(1)} %get-tuple-element.108), channel_id=1, source_target_pairs={{0,2},{1,3},{2,4},{3,5},{4,6},{5,7},{6,0},{7,1},{8,10},{9,11},{10,... | collective-permute-start | bytes 294920 | tf_op jit(solution)/shard_map/while/body/eval_jaxpr/ppermute | solution.py:60
  171.1 8.4 %collective-permute-start.17 = (f32[96,256]{1,0:T(8,128)S(1)}, f32[96,256]{1,0:T(8,128)S(1)}, u32[]{:S(2)}, u32[]{:S(2)}) collective-permute-start(f32[96,256]{1,0:T(8,128)S(1)} %get-tuple-element.109), channel_id=1, source_target_pairs={{0,4},{1,5},{2,6},{3,7},{4,0},{5,1},{6,2},{7,3},{8,12},{9,13},{10,... | collective-permute-start | bytes 294920 | tf_op jit(solution)/shard_map/while/body/eval_jaxpr/ppermute | solution.py:60
  172.3 7.2 %collective-permute-start.18 = (f32[96,256]{1,0:T(8,128)S(1)}, f32[96,256]{1,0:T(8,128)S(1)}, u32[]{:S(2)}, u32[]{:S(2)}) collective-permute-start(f32[96,256]{1,0:T(8,128)S(1)} %get-tuple-element.110), channel_id=1, source_target_pairs={{0,6},{1,7},{2,0},{3,1},{4,2},{5,3},{6,4},{7,5},{8,14},{9,15},{10,... | collective-permute-start | bytes 294920 | tf_op jit(solution)/shard_map/while/body/eval_jaxpr/ppermute | solution.py:60
  179.5 10.6 %collective-permute-start.3 = (f32[96,256]{1,0:T(8,128)S(1)}, f32[96,256]{1,0:T(8,128)S(1)}, u32[]{:S(2)}, u32[]{:S(2)}) collective-permute-start(f32[96,256]{1,0:T(8,128)S(1)} %copy.17), channel_id=1, source_target_pairs={{0,32},{1,33},{2,34},{3,35},{4,36},{5,37},{6,38},{7,39},{8,40},{9,... | collective-permute-start | bytes 294920 | tf_op jit(solution)/shard_map/while/body/eval_jaxpr/ppermute | solution.py:60
  187.9 18.1 %collective-permute-start.7 = (f32[384,256]{1,0:T(8,128)S(1)}, f32[384,256]{1,0:T(8,128)S(1)}, u32[]{:S(2)}, u32[]{:S(2)}) collective-permute-start(f32[384,256]{1,0:T(8,128)S(1)} %constant_dynamic-update-slice_fusion.19.refs_1_), channel_id=1, source_target_pairs={{0,64},{1,9},{2,66},{3,11},{4,68},{5,13},{6,70},{7,15},{8,72},{9,1... | collective-permute-start | bytes 1179656 | tf_op jit(solution)/shard_map/while/body/eval_jaxpr/ppermute | solution.py:60
  190.0 16.0 %collective-permute-start.8 = (f32[384,256]{1,0:T(8,128)S(1)}, f32[384,256]{1,0:T(8,128)S(1)}, u32[]{:S(2)}, u32[]{:S(2)}) collective-permute-start(f32[384,256]{1,0:T(8,128)S(1)} %constant_dynamic-update-slice_fusion.19.refs_1_), channel_id=1, source_target_pairs={{0,192},{1,25},{2,194},{3,27},{4,196},{5,29},{6,198},{7,31},{8,200... | collective-permute-start | bytes 1179656 | tf_op jit(solution)/shard_map/while/body/eval_jaxpr/ppermute | solution.py:60
  191.0 7.0 %collective-permute-start.5 = (f32[96,256]{1,0:T(8,128)S(1)}, f32[96,256]{1,0:T(8,128)S(1)}, u32[]{:S(2)}, u32[]{:S(2)}) collective-permute-start(f32[96,256]{1,0:T(8,128)S(1)} %collective-permute-done.3), channel_id=1, source_target_pairs={{0,16},{1,129},{2,18},{3,131},{4,20},{5,133},{6,22},{7,135},{8,24}... | collective-permute-start | bytes 294920 | tf_op jit(solution)/shard_map/while/body/eval_jaxpr/ppermute | solution.py:60
  198.8 10.8 %collective-permute-start.10 = (f32[384,256]{1,0:T(8,128)S(1)}, f32[384,256]{1,0:T(8,128)S(1)}, u32[]{:S(2)}, u32[]{:S(2)}) collective-permute-start(f32[384,256]{1,0:T(8,128)S(1)} %constant_dynamic-update-slice_fusion.23.refs_2_), channel_id=1, source_target_pairs={{0,192},{1,25},{2,194},{3,27},{4,196},{5,29},{6,198},{7,31},{8,200... | collective-permute-start | bytes 1179656 | tf_op jit(solution)/shard_map/while/body/eval_jaxpr/ppermute | solution.py:60
  202.2 7.8 %collective-permute-start.9 = (f32[384,256]{1,0:T(8,128)S(1)}, f32[384,256]{1,0:T(8,128)S(1)}, u32[]{:S(2)}, u32[]{:S(2)}) collective-permute-start(f32[384,256]{1,0:T(8,128)S(1)} %constant_dynamic-update-slice_fusion.23.refs_2_), channel_id=1, source_target_pairs={{0,64},{1,9},{2,66},{3,11},{4,68},{5,13},{6,70},{7,15},{8,72},{9,1... | collective-permute-start | bytes 1179656 | tf_op jit(solution)/shard_map/while/body/eval_jaxpr/ppermute | solution.py:60
  206.1 7.2 %collective-permute-start.13 = (f32[192,256]{1,0:T(8,128)S(1)}, f32[192,256]{1,0:T(8,128)S(1)}, u32[]{:S(2)}, u32[]{:S(2)}) collective-permute-start(f32[192,256]{1,0:T(8,128)S(1)} %slice.54), channel_id=1, source_target_pairs={{0,64},{1,9},{2,66},{3,11},{4,68},{5,13},{6,70},{7,15},{8,72},{9,1... | collective-permute-start | bytes 589832 | tf_op jit(solution)/shard_map/while/body/eval_jaxpr/ppermute | solution.py:60
  210.0 6.9 %collective-permute-start.11 = (f32[192,256]{1,0:T(8,128)S(1)}, f32[192,256]{1,0:T(8,128)S(1)}, u32[]{:S(2)}, u32[]{:S(2)}) collective-permute-start(f32[192,256]{1,0:T(8,128)S(1)} %slice.52), channel_id=1, source_target_pairs={{0,64},{1,9},{2,66},{3,11},{4,68},{5,13},{6,70},{7,15},{8,72},{9,1... | collective-permute-start | bytes 589832 | tf_op jit(solution)/shard_map/while/body/eval_jaxpr/ppermute | solution.py:60
  221.3 7.6 %collective-permute-start.16 = (f32[96,256]{1,0:T(8,128)S(1)}, f32[96,256]{1,0:T(8,128)S(1)}, u32[]{:S(2)}, u32[]{:S(2)}) collective-permute-start(f32[96,256]{1,0:T(8,128)S(1)} %get-tuple-element.108), channel_id=1, source_target_pairs={{0,2},{1,3},{2,4},{3,5},{4,6},{5,7},{6,0},{7,1},{8,10},{9,11},{10,... | collective-permute-start | bytes 294920 | tf_op jit(solution)/shard_map/while/body/eval_jaxpr/ppermute | solution.py:60
  224.0 8.4 %collective-permute-start.17 = (f32[96,256]{1,0:T(8,128)S(1)}, f32[96,256]{1,0:T(8,128)S(1)}, u32[]{:S(2)}, u32[]{:S(2)}) collective-permute-start(f32[96,256]{1,0:T(8,128)S(1)} %get-tuple-element.109), channel_id=1, source_target_pairs={{0,4},{1,5},{2,6},{3,7},{4,0},{5,1},{6,2},{7,3},{8,12},{9,13},{10,... | collective-permute-start | bytes 294920 | tf_op jit(solution)/shard_map/while/body/eval_jaxpr/ppermute | solution.py:60
  225.3 7.1 %collective-permute-start.18 = (f32[96,256]{1,0:T(8,128)S(1)}, f32[96,256]{1,0:T(8,128)S(1)}, u32[]{:S(2)}, u32[]{:S(2)}) collective-permute-start(f32[96,256]{1,0:T(8,128)S(1)} %get-tuple-element.110), channel_id=1, source_target_pairs={{0,6},{1,7},{2,0},{3,1},{4,2},{5,3},{6,4},{7,5},{8,14},{9,15},{10,... | collective-permute-start | bytes 294920 | tf_op jit(solution)/shard_map/while/body/eval_jaxpr/ppermute | solution.py:60
  232.5 15.8 %collective-permute-start.3 = (f32[96,256]{1,0:T(8,128)S(1)}, f32[96,256]{1,0:T(8,128)S(1)}, u32[]{:S(2)}, u32[]{:S(2)}) collective-permute-start(f32[96,256]{1,0:T(8,128)S(1)} %copy.17), channel_id=1, source_target_pairs={{0,32},{1,33},{2,34},{3,35},{4,36},{5,37},{6,38},{7,39},{8,40},{9,... | collective-permute-start | bytes 294920 | tf_op jit(solution)/shard_map/while/body/eval_jaxpr/ppermute | solution.py:60
  246.1 18.1 %collective-permute-start.7 = (f32[384,256]{1,0:T(8,128)S(1)}, f32[384,256]{1,0:T(8,128)S(1)}, u32[]{:S(2)}, u32[]{:S(2)}) collective-permute-start(f32[384,256]{1,0:T(8,128)S(1)} %constant_dynamic-update-slice_fusion.19.refs_1_), channel_id=1, source_target_pairs={{0,64},{1,9},{2,66},{3,11},{4,68},{5,13},{6,70},{7,15},{8,72},{9,1... | collective-permute-start | bytes 1179656 | tf_op jit(solution)/shard_map/while/body/eval_jaxpr/ppermute | solution.py:60
  248.1 16.0 %collective-permute-start.8 = (f32[384,256]{1,0:T(8,128)S(1)}, f32[384,256]{1,0:T(8,128)S(1)}, u32[]{:S(2)}, u32[]{:S(2)}) collective-permute-start(f32[384,256]{1,0:T(8,128)S(1)} %constant_dynamic-update-slice_fusion.19.refs_1_), channel_id=1, source_target_pairs={{0,192},{1,25},{2,194},{3,27},{4,196},{5,29},{6,198},{7,31},{8,200... | collective-permute-start | bytes 1179656 | tf_op jit(solution)/shard_map/while/body/eval_jaxpr/ppermute | solution.py:60
  249.1 7.0 %collective-permute-start.5 = (f32[96,256]{1,0:T(8,128)S(1)}, f32[96,256]{1,0:T(8,128)S(1)}, u32[]{:S(2)}, u32[]{:S(2)}) collective-permute-start(f32[96,256]{1,0:T(8,128)S(1)} %collective-permute-done.3), channel_id=1, source_target_pairs={{0,16},{1,129},{2,18},{3,131},{4,20},{5,133},{6,22},{7,135},{8,24}... | collective-permute-start | bytes 294920 | tf_op jit(solution)/shard_map/while/body/eval_jaxpr/ppermute | solution.py:60
  256.9 10.8 %collective-permute-start.10 = (f32[384,256]{1,0:T(8,128)S(1)}, f32[384,256]{1,0:T(8,128)S(1)}, u32[]{:S(2)}, u32[]{:S(2)}) collective-permute-start(f32[384,256]{1,0:T(8,128)S(1)} %constant_dynamic-update-slice_fusion.23.refs_2_), channel_id=1, source_target_pairs={{0,192},{1,25},{2,194},{3,27},{4,196},{5,29},{6,198},{7,31},{8,200... | collective-permute-start | bytes 1179656 | tf_op jit(solution)/shard_map/while/body/eval_jaxpr/ppermute | solution.py:60
  260.3 7.8 %collective-permute-start.9 = (f32[384,256]{1,0:T(8,128)S(1)}, f32[384,256]{1,0:T(8,128)S(1)}, u32[]{:S(2)}, u32[]{:S(2)}) collective-permute-start(f32[384,256]{1,0:T(8,128)S(1)} %constant_dynamic-update-slice_fusion.23.refs_2_), channel_id=1, source_target_pairs={{0,64},{1,9},{2,66},{3,11},{4,68},{5,13},{6,70},{7,15},{8,72},{9,1... | collective-permute-start | bytes 1179656 | tf_op jit(solution)/shard_map/while/body/eval_jaxpr/ppermute | solution.py:60
  264.2 7.2 %collective-permute-start.13 = (f32[192,256]{1,0:T(8,128)S(1)}, f32[192,256]{1,0:T(8,128)S(1)}, u32[]{:S(2)}, u32[]{:S(2)}) collective-permute-start(f32[192,256]{1,0:T(8,128)S(1)} %slice.54), channel_id=1, source_target_pairs={{0,64},{1,9},{2,66},{3,11},{4,68},{5,13},{6,70},{7,15},{8,72},{9,1... | collective-permute-start | bytes 589832 | tf_op jit(solution)/shard_map/while/body/eval_jaxpr/ppermute | solution.py:60
  265.7 6.9 %collective-permute-start.14 = (f32[192,256]{1,0:T(8,128)S(1)}, f32[192,256]{1,0:T(8,128)S(1)}, u32[]{:S(2)}, u32[]{:S(2)}) collective-permute-start(f32[192,256]{1,0:T(8,128)S(1)} %slice.55), channel_id=1, source_target_pairs={{0,192},{1,25},{2,194},{3,27},{4,196},{5,29},{6,198},{7,31},{8,200... | collective-permute-start | bytes 589832 | tf_op jit(solution)/shard_map/while/body/eval_jaxpr/ppermute | solution.py:60
  279.4 7.6 %collective-permute-start.16 = (f32[96,256]{1,0:T(8,128)S(1)}, f32[96,256]{1,0:T(8,128)S(1)}, u32[]{:S(2)}, u32[]{:S(2)}) collective-permute-start(f32[96,256]{1,0:T(8,128)S(1)} %get-tuple-element.108), channel_id=1, source_target_pairs={{0,2},{1,3},{2,4},{3,5},{4,6},{5,7},{6,0},{7,1},{8,10},{9,11},{10,... | collective-permute-start | bytes 294920 | tf_op jit(solution)/shard_map/while/body/eval_jaxpr/ppermute | solution.py:60
  282.1 8.4 %collective-permute-start.17 = (f32[96,256]{1,0:T(8,128)S(1)}, f32[96,256]{1,0:T(8,128)S(1)}, u32[]{:S(2)}, u32[]{:S(2)}) collective-permute-start(f32[96,256]{1,0:T(8,128)S(1)} %get-tuple-element.109), channel_id=1, source_target_pairs={{0,4},{1,5},{2,6},{3,7},{4,0},{5,1},{6,2},{7,3},{8,12},{9,13},{10,... | collective-permute-start | bytes 294920 | tf_op jit(solution)/shard_map/while/body/eval_jaxpr/ppermute | solution.py:60
  283.4 7.1 %collective-permute-start.18 = (f32[96,256]{1,0:T(8,128)S(1)}, f32[96,256]{1,0:T(8,128)S(1)}, u32[]{:S(2)}, u32[]{:S(2)}) collective-permute-start(f32[96,256]{1,0:T(8,128)S(1)} %get-tuple-element.110), channel_id=1, source_target_pairs={{0,6},{1,7},{2,0},{3,1},{4,2},{5,3},{6,4},{7,5},{8,14},{9,15},{10,... | collective-permute-start | bytes 294920 | tf_op jit(solution)/shard_map/while/body/eval_jaxpr/ppermute | solution.py:60
  290.6 10.8 %collective-permute-start.3 = (f32[96,256]{1,0:T(8,128)S(1)}, f32[96,256]{1,0:T(8,128)S(1)}, u32[]{:S(2)}, u32[]{:S(2)}) collective-permute-start(f32[96,256]{1,0:T(8,128)S(1)} %copy.17), channel_id=1, source_target_pairs={{0,32},{1,33},{2,34},{3,35},{4,36},{5,37},{6,38},{7,39},{8,40},{9,... | collective-permute-start | bytes 294920 | tf_op jit(solution)/shard_map/while/body/eval_jaxpr/ppermute | solution.py:60
  299.1 17.9 %collective-permute-start.7 = (f32[384,256]{1,0:T(8,128)S(1)}, f32[384,256]{1,0:T(8,128)S(1)}, u32[]{:S(2)}, u32[]{:S(2)}) collective-permute-start(f32[384,256]{1,0:T(8,128)S(1)} %constant_dynamic-update-slice_fusion.19.refs_1_), channel_id=1, source_target_pairs={{0,64},{1,9},{2,66},{3,11},{4,68},{5,13},{6,70},{7,15},{8,72},{9,1... | collective-permute-start | bytes 1179656 | tf_op jit(solution)/shard_map/while/body/eval_jaxpr/ppermute | solution.py:60
  301.2 15.9 %collective-permute-start.8 = (f32[384,256]{1,0:T(8,128)S(1)}, f32[384,256]{1,0:T(8,128)S(1)}, u32[]{:S(2)}, u32[]{:S(2)}) collective-permute-start(f32[384,256]{1,0:T(8,128)S(1)} %constant_dynamic-update-slice_fusion.19.refs_1_), channel_id=1, source_target_pairs={{0,192},{1,25},{2,194},{3,27},{4,196},{5,29},{6,198},{7,31},{8,200... | collective-permute-start | bytes 1179656 | tf_op jit(solution)/shard_map/while/body/eval_jaxpr/ppermute | solution.py:60
  302.0 7.1 %collective-permute-start.5 = (f32[96,256]{1,0:T(8,128)S(1)}, f32[96,256]{1,0:T(8,128)S(1)}, u32[]{:S(2)}, u32[]{:S(2)}) collective-permute-start(f32[96,256]{1,0:T(8,128)S(1)} %collective-permute-done.3), channel_id=1, source_target_pairs={{0,16},{1,129},{2,18},{3,131},{4,20},{5,133},{6,22},{7,135},{8,24}... | collective-permute-start | bytes 294920 | tf_op jit(solution)/shard_map/while/body/eval_jaxpr/ppermute | solution.py:60
  309.8 10.8 %collective-permute-start.10 = (f32[384,256]{1,0:T(8,128)S(1)}, f32[384,256]{1,0:T(8,128)S(1)}, u32[]{:S(2)}, u32[]{:S(2)}) collective-permute-start(f32[384,256]{1,0:T(8,128)S(1)} %constant_dynamic-update-slice_fusion.23.refs_2_), channel_id=1, source_target_pairs={{0,192},{1,25},{2,194},{3,27},{4,196},{5,29},{6,198},{7,31},{8,200... | collective-permute-start | bytes 1179656 | tf_op jit(solution)/shard_map/while/body/eval_jaxpr/ppermute | solution.py:60
  313.2 7.8 %collective-permute-start.9 = (f32[384,256]{1,0:T(8,128)S(1)}, f32[384,256]{1,0:T(8,128)S(1)}, u32[]{:S(2)}, u32[]{:S(2)}) collective-permute-start(f32[384,256]{1,0:T(8,128)S(1)} %constant_dynamic-update-slice_fusion.23.refs_2_), channel_id=1, source_target_pairs={{0,64},{1,9},{2,66},{3,11},{4,68},{5,13},{6,70},{7,15},{8,72},{9,1... | collective-permute-start | bytes 1179656 | tf_op jit(solution)/shard_map/while/body/eval_jaxpr/ppermute | solution.py:60
  317.1 7.2 %collective-permute-start.13 = (f32[192,256]{1,0:T(8,128)S(1)}, f32[192,256]{1,0:T(8,128)S(1)}, u32[]{:S(2)}, u32[]{:S(2)}) collective-permute-start(f32[192,256]{1,0:T(8,128)S(1)} %slice.54), channel_id=1, source_target_pairs={{0,64},{1,9},{2,66},{3,11},{4,68},{5,13},{6,70},{7,15},{8,72},{9,1... | collective-permute-start | bytes 589832 | tf_op jit(solution)/shard_map/while/body/eval_jaxpr/ppermute | solution.py:60
  332.4 7.6 %collective-permute-start.16 = (f32[96,256]{1,0:T(8,128)S(1)}, f32[96,256]{1,0:T(8,128)S(1)}, u32[]{:S(2)}, u32[]{:S(2)}) collective-permute-start(f32[96,256]{1,0:T(8,128)S(1)} %get-tuple-element.108), channel_id=1, source_target_pairs={{0,2},{1,3},{2,4},{3,5},{4,6},{5,7},{6,0},{7,1},{8,10},{9,11},{10,... | collective-permute-start | bytes 294920 | tf_op jit(solution)/shard_map/while/body/eval_jaxpr/ppermute | solution.py:60
  335.0 8.4 %collective-permute-start.17 = (f32[96,256]{1,0:T(8,128)S(1)}, f32[96,256]{1,0:T(8,128)S(1)}, u32[]{:S(2)}, u32[]{:S(2)}) collective-permute-start(f32[96,256]{1,0:T(8,128)S(1)} %get-tuple-element.109), channel_id=1, source_target_pairs={{0,4},{1,5},{2,6},{3,7},{4,0},{5,1},{6,2},{7,3},{8,12},{9,13},{10,... | collective-permute-start | bytes 294920 | tf_op jit(solution)/shard_map/while/body/eval_jaxpr/ppermute | solution.py:60
  336.4 7.1 %collective-permute-start.18 = (f32[96,256]{1,0:T(8,128)S(1)}, f32[96,256]{1,0:T(8,128)S(1)}, u32[]{:S(2)}, u32[]{:S(2)}) collective-permute-start(f32[96,256]{1,0:T(8,128)S(1)} %get-tuple-element.110), channel_id=1, source_target_pairs={{0,6},{1,7},{2,0},{3,1},{4,2},{5,3},{6,4},{7,5},{8,14},{9,15},{10,... | collective-permute-start | bytes 294920 | tf_op jit(solution)/shard_map/while/body/eval_jaxpr/ppermute | solution.py:60
  (55 other events, 326.0 us)

commit v2 on v0

v2 whole, which is shorter than its diff:
```python
import functools

import jax
import jax.numpy as jnp
from jax import lax
from jax.experimental import pallas as pl
from jax.experimental.pallas import tpu as pltpu
from jax.sharding import Mesh, PartitionSpec as P


ORDER = 24576
VECS = 256
DEGREE = 6
SH = 96
LOCAL = 768
COLS = 3072

filter_center = 2.75
filter_half = 1.75
filter_lower = 0.0


AX = ("x", "zh", "y", "zl", "core")
DIMS = (4, 2, 4, 4, 2)


def lin(x, zh, y, zl, core):
    return (((x * 2 + zh) * 4 + y) * 4 + zl) * 2 + core


def pairs(move):
    out = []
    for x in range(4):
        for zh in range(2):
            for y in range(4):
                for zl in range(4):
                    for core in range(2):
                        out.append((lin(x, zh, y, zl, core), lin(*move(x, zh, y, zl, core))))
    return out


SWAP_CORE = pairs(lambda x, zh, y, zl, core: (x, zh, y, zl, 1 - core))
SWAP_ZH = pairs(lambda x, zh, y, zl, core: (x, 1 - zh, y, zl, core))


def along_y(x, zh, y, zl, core, s):
    return (x, zh, (y + s) % 4, zl, core)


def along_x(x, zh, y, zl, core, s):
    return ((x + s) % 4, zh, y, zl, core)


FIRST = [pairs(lambda x, zh, y, zl, core, s=s: (along_x if core else along_y)(x, zh, y, zl, core, s)) for s in range(4)]
SECOND = [pairs(lambda x, zh, y, zl, core, s=s: (along_y if core else along_x)(x, zh, y, zl, core, s)) for s in range(4)]
ALONG_ZL = [pairs(lambda x, zh, y, zl, core, s=s: (x, zh, y, (zl + s) % 4, core)) for s in range(4)]


def send(value, moves):
    return lax.ppermute(value, AX, moves)


HALF = 4 * SH
BLOCKS = 4
WIDE = COLS // BLOCKS
LANES = 128


def position():
    x, zh, y, zl, core = (lax.axis_index(a) for a in AX)
    return core, zl, zh, jnp.where(core == 0, x, y), jnp.where(core == 0, y, x)


def split_kernel(h_ref, out_ref):
    core = position()[0]

    def write(order):
        h = h_ref[...]
        for block in range(BLOCKS):
            part = jnp.concatenate([h[:, i * SH : (i + 1) * SH] for i in order[8 * block : 8 * block + 8]], axis=1)
            hi = part.astype(jnp.bfloat16)
            out_ref[block, :, :WIDE] = hi
            out_ref[block, :, WIDE:] = (part - hi.astype(jnp.float32)).astype(jnp.bfloat16)

    @pl.when(core == 0)
    def _():
        write(list(range(32)))

    @pl.when(core != 0)
    def _():
        write([(x * 2 + zh) * 4 + y for y in range(4) for zh in range(2) for x in range(4)])


def split_operator(coupling):
    return pl.pallas_call(
        split_kernel,
        grid=(LOCAL // 96,),
        in_specs=[pl.BlockSpec((96, COLS), lambda i: (i, 0))],
        out_specs=pl.BlockSpec((BLOCKS, 96, 2 * WIDE), lambda i: (0, i, 0)),
        out_shape=jax.ShapeDtypeStruct((BLOCKS, LOCAL, 2 * WIDE), jnp.bfloat16),
        compiler_params=pltpu.CompilerParams(vmem_limit_bytes=16 << 20),
    )(coupling)


def product_kernel(steps, has_acc, last, *refs):
    operator, refs = refs[0], refs[1:]
    parts, refs = refs[: len(steps)], refs[len(steps) :]
    acc_in, refs = (refs[0], refs[1:]) if has_acc else (None, refs)
    outs, rows_of = refs[:-1], refs[-1]
    core, zl, zh, own_u, own_v = position()
    for b, part in enumerate(parts):
        for s in range(4):
            for z in range(2):
                rows = part[(s * 2 + z) * SH : (s * 2 + z + 1) * SH, :]
                hi = rows.astype(jnp.bfloat16)
                lo = (rows - hi.astype(jnp.float32)).astype(jnp.bfloat16)
                at = pl.multiple_of(((zh + z) % 2) * HALF + ((own_v - s + 4) % 4) * SH, SH)
                rows_of[b, pl.ds(at, SH), :LANES] = hi
                rows_of[b, pl.ds(at, SH), LANES:] = lo
    for half in range(2):
        m = slice(half * LOCAL // 2, (half + 1) * LOCAL // 2)
        acc = acc_in[m, :] if has_acc else None
        for b, t in enumerate(steps):
            block = (own_u - t + 4) % 4
            both = jnp.dot(operator[block, m, :WIDE], rows_of[b], preferred_element_type=jnp.float32)
            term = jnp.dot(operator[block, m, WIDE:], rows_of[b, :, :LANES], preferred_element_type=jnp.float32)
            term += both[:, LANES:]
            term += both[:, :LANES]
            acc = term if acc is None else acc + term
        if not last:
            outs[0][m, :] = acc
            continue
        keep, give = outs
        for pair in range(2):
            to = pl.multiple_of(((half * 2 + pair - zl + 4) % 4) * SH, SH)
            even, odd = acc[pair * 2 * SH : pair * 2 * SH + SH], acc[pair * 2 * SH + SH : (pair + 1) * 2 * SH]

            @pl.when(core == 0)
            def _():
                keep[pl.ds(to, SH), :] = even
                give[pl.ds(to, SH), :] = odd

            @pl.when(core != 0)
            def _():
                keep[pl.ds(to, SH), :] = odd
                give[pl.ds(to, SH), :] = even


def product(operator, parts, acc, last=False):
    vmem = pl.BlockSpec(memory_space=pltpu.VMEM)
    args = [operator, *parts.values()] + ([] if acc is None else [acc])
    shape = [(HALF, LANES)] * 2 if last else [(LOCAL, LANES)]
    out = pl.pallas_call(
        functools.partial(product_kernel, tuple(parts), acc is not None, last),
        in_specs=[vmem] * len(args),
        out_specs=[vmem] * len(shape),
        out_shape=[jax.ShapeDtypeStruct(a, jnp.float32) for a in shape],
        scratch_shapes=[pltpu.VMEM((len(parts), WIDE, 2 * LANES), jnp.bfloat16)],
        compiler_params=pltpu.CompilerParams(vmem_limit_bytes=16 << 20),
    )(*args)
    return out if last else out[0]


def on_device(coupling, vectors):
    core = lax.axis_index("core")
    operator = split_operator(coupling)

    def gather(current):
        partner = send(current, SWAP_ZH)
        plane = jnp.concatenate([current, partner], axis=0)
        near = {s: send(plane, FIRST[s]) for s in (2, 1, 3)}
        first = jnp.concatenate([plane, near[1], near[2], near[3]], axis=0)
        return first, {s: send(first, SECOND[s]) for s in (2, 1, 3)}

    def apply(current):
        first, far = gather(current)
        acc = product(operator, {0: first}, None)
        acc = product(operator, {1: far[1], 3: far[3]}, acc)
        keep, give = product(operator, {2: far[2]}, acc, last=True)
        total = keep + send(give, SWAP_CORE)
        here = {s: send(total[s * SH : (s + 1) * SH], ALONG_ZL[s]) for s in (2, 1, 3)}
        return (total[:SH] + here[1]) + (here[2] + here[3])

    streams = lax.optimization_barrier((vectors[:, :LANES], vectors[:, LANES:]))
    states = [(v, v) for v in streams]
    sigma_first = filter_half / (filter_lower - filter_center)
    sigma_now = sigma_first
    for degree_index in range(DEGREE):
        sigma_new = 1.0 / (2.0 / sigma_first - sigma_now)
        gain, loss = 2.0 * sigma_new / filter_half, sigma_now * sigma_new
        if degree_index == 0:
            sigma_new, gain, loss = sigma_first, sigma_first / filter_half, None
        for i, (previous, current) in enumerate(states):
            following = gain * (apply(current) - filter_center * current)
            if loss is not None:
                following = following - loss * previous
            states[i] = (current, following)
        sigma_now = sigma_new
    current = jnp.concatenate([following for _, following in states], axis=1)

    local = jnp.dot(current.T, current, precision=lax.Precision.HIGHEST, preferred_element_type=jnp.float32)
    halves = local.reshape(2, 128, VECS)
    mine = lax.dynamic_index_in_dim(halves, core, 0, keepdims=False)
    other = lax.dynamic_index_in_dim(halves, 1 - core, 0, keepdims=False)
    half = mine + send(other, SWAP_CORE)
    piece = lax.all_to_all(half.reshape(16, 8, VECS), ("x", "y"), 0, 0).sum(axis=0)
    every = lax.all_to_all(jnp.broadcast_to(piece, (8, 8, VECS)), ("zh", "zl"), 0, 0).sum(axis=0) / ORDER
    half = lax.all_to_all(jnp.broadcast_to(every, (16, 8, VECS)), ("x", "y"), 0, 0).reshape(128, VECS)
    other = send(half, SWAP_CORE)
    gram = jnp.concatenate([jnp.where(core == 0, half, other), jnp.where(core == 0, other, half)], axis=0)
    return current, gram


def solution(mesh):
    fine = Mesh(mesh.devices.reshape(DIMS), AX)
    return jax.shard_map(
        on_device,
        mesh=fine,
        in_specs=(P(("x", "zh", "y"), ("zl", "core")), P(AX, None)),
        out_specs=(P(AX, None), P()),
        check_vma=False,
    )
```

time: 404 us -> 379 us (0.938)
  waiting for transfers between devices: 145 us -> 44.6 us
  starting transfers between devices: 158 us -> 234 us
  Pallas kernels: 54 us -> 46.5 us
    ppermute x104 -> x134, waiting for transfers between devices: 145 us -> 44.6 us  [send(): return lax.ppermute(value, AX, moves)]
    ppermute x104 -> x134, starting transfers between devices: 158 us -> 234 us  [send(): return lax.ppermute(value, AX, moves)]
    pallas_call x24 -> x36, Pallas kernels: 47.9 us -> 41.4 us  [product(): pl.pallas_call(functools.partial(product_kernel, tuple(parts), acc is not...]
  transfers between devices with their start and end apart: 104 -> 134, of which waited for: 70 -> 22; matrix products, arithmetic and copies ran while one was open for 0% -> 0% of each run, Pallas kernels for 11% -> 12%
where the time goes in v2:
time: 379 us; the launch traced here: 372 us
  starting transfers between devices  234 us (62%)
  Pallas kernels  46.5 us (12%)
  waiting for transfers between devices  44.6 us (12%)
  blocking collectives  33.9 us (9%)
  local copies, waits for them, and re-layouts  8.78 us (2%)
    ppermute x134, starting transfers between devices, send(): return lax.ppermute(value, AX, moves)  234 us
    ppermute x134, waiting for transfers between devices, send(): return lax.ppermute(value, AX, moves)  44.6 us
    pallas_call x36, Pallas kernels, product(): pl.pallas_call(functools.partial(product_kernel, tuple(parts), acc is not...  41.4 us
    all_to_all x1, blocking collectives, on_device(): lax.all_to_all(half.reshape(16, 8, VECS), ('x', 'y'), 0, 0).sum(axis=0)  12.4 us
    all_to_all x1, blocking collectives, on_device(): lax.all_to_all(jnp.broadcast_to(piece, (8, 8, VECS)), ('zh', 'zl'), 0, 0)  11.3 us
    all_to_all x1, blocking collectives, on_device(): lax.all_to_all(jnp.broadcast_to(every, (16, 8, VECS)), ('x', 'y'), 0, 0)  10.2 us
    unnamed x44, local copies, waits for them, and re-layouts  7.64 us
  transfers between devices with their start and end apart: 134, of which 22 were waited for; matrix products, arithmetic and copies ran while one was open for 0% of the time, Pallas kernels for 12%

profile of v2, /device:TPU:1, one launch (start us, length us, event | category | flops | bytes accessed | tf_op | source)
XLA Modules:
  0.0 371.8 jit_solution(6935934037156425189)
XLA Ops:
  1.5 7.8 %collective-permute-start = (f32[96,128]{1,0:T(8,128)S(1)}, f32[96,128]{1,0:T(8,128)S(1)}, u32[]{:S(2)}, u32[]{:S(2)}) collective-permute-start(f32[96,128]{1,0:T(8,128)S(1)} %get-tuple-element.28), channel_id=1, source_target_pairs={{0,32},{1,33},{2,34},{3,35},{4,36},{5,37},{6,38},{7,39},{8,40},{9,... | collective-permute-start | bytes 147464 | tf_op jit(solution)/shard_map/ppermute | solution.py:60
  12.0 2.5 collective-permute-start.2
  19.3 2.3 collective-permute-start.68
  30.3 3.7 copy-done.2
  34.0 5.0 %shard_map.41.refs_0_ = bf16[4,768,1536]{2,1,0:T(8,128)(2,1)S(1)} custom-call(f32[768,3072]{1,0:T(8,128)S(1)} %copy-done.2), custom_call_target="tpu_custom_call" | custom-call | tf_op jit(solution)/shard_map/pallas_call | solution.py:95
  42.5 6.6 %collective-permute-start.7 = (f32[384,128]{1,0:T(8,128)S(1)}, f32[384,128]{1,0:T(8,128)S(1)}, u32[]{:S(2)}, u32[]{:S(2)}) collective-permute-start(f32[384,128]{1,0:T(8,128)S(1)} %get-tuple-element.30), channel_id=1, source_target_pairs={{0,1},{1,0},{2,3},{3,2},{4,5},{5,4},{6,7},{7,6},{8,9},{9,8},{10,11... | collective-permute-start | bytes 589832 | tf_op jit(solution)/shard_map/ppermute | solution.py:60
  52.8 3.2 collective-permute-start.10
  56.6 3.0 collective-permute-start.74
  59.6 2.2 collective-permute-start.76
  61.8 5.3 %collective-permute-start.11 = (f32[96,128]{1,0:T(8,128)S(1)}, f32[96,128]{1,0:T(8,128)S(1)}, u32[]{:S(2)}, u32[]{:S(2)}) collective-permute-start(f32[96,128]{1,0:T(8,128)S(1)} %get-tuple-element.62), channel_id=1, source_target_pairs={{0,32},{1,33},{2,34},{3,35},{4,36},{5,37},{6,38},{7,39},{8,40},{9,... | collective-permute-start | bytes 147464 | tf_op jit(solution)/shard_map/ppermute | solution.py:60
  67.1 3.5 collective-permute-start.77
  70.7 2.4 collective-permute-start.13
  75.0 2.3 collective-permute-start.79
  78.2 2.7 collective-permute-start.16
  83.2 2.5 collective-permute-start.82
  86.0 3.2 collective-permute-done.16.refs_1_
  89.1 1.9 collective-permute-start.81
  95.9 6.9 %collective-permute-start.18 = (f32[384,128]{1,0:T(8,128)S(1)}, f32[384,128]{1,0:T(8,128)S(1)}, u32[]{:S(2)}, u32[]{:S(2)}) collective-permute-start(f32[384,128]{1,0:T(8,128)S(1)} %get-tuple-element.32), channel_id=1, source_target_pairs={{0,1},{1,0},{2,3},{3,2},{4,5},{5,4},{6,7},{7,6},{8,9},{9,8},{10,11... | collective-permute-start | bytes 589832 | tf_op jit(solution)/shard_map/ppermute | solution.py:60
  106.3 3.4 collective-permute-start.84
  110.2 2.9 collective-permute-start.21
  114.9 2.2 collective-permute-start.87
  117.1 4.7 %collective-permute-start.22 = (f32[96,128]{1,0:T(8,128)S(1)}, f32[96,128]{1,0:T(8,128)S(1)}, u32[]{:S(2)}, u32[]{:S(2)}) collective-permute-start(f32[96,128]{1,0:T(8,128)S(1)} %get-tuple-element.61), channel_id=1, source_target_pairs={{0,32},{1,33},{2,34},{3,35},{4,36},{5,37},{6,38},{7,39},{8,40},{9,... | collective-permute-start | bytes 147464 | tf_op jit(solution)/shard_map/ppermute | solution.py:60
  121.8 4.1 %collective-permute-start.88 = (f32[96,128]{1,0:T(8,128)S(1)}, f32[96,128]{1,0:T(8,128)S(1)}, u32[]{:S(2)}, u32[]{:S(2)}) collective-permute-start(f32[96,128]{1,0:T(8,128)S(1)} %get-tuple-element.71), channel_id=1, source_target_pairs={{0,32},{1,33},{2,34},{3,35},{4,36},{5,37},{6,38},{7,39},{8,40},{9,... | collective-permute-start | bytes 147464 | tf_op jit(solution)/shard_map/ppermute | solution.py:60
  126.0 4.6 %collective-permute-start.24 = (f32[192,128]{1,0:T(8,128)S(1)}, f32[192,128]{1,0:T(8,128)S(1)}, u32[]{:S(2)}, u32[]{:S(2)}) collective-permute-start(f32[192,128]{1,0:T(8,128)S(1)} %pad_maximum_fusion.2), channel_id=1, source_target_pairs={{0,16},{1,129},{2,18},{3,131},{4,20},{5,133},{6,22},{7,135},{8,24}... | collective-permute-start | bytes 294920 | tf_op jit(solution)/shard_map/ppermute | solution.py:60
  135.3 2.7 collective-permute-start.28
  138.8 2.2 collective-permute-start.94
  141.0 6.7 %collective-permute-done.27.refs_1_ = f32[768,128]{1,0:T(8,128)S(1)} collective-permute-done((f32[768,128]{1,0:T(8,128)S(1)}, f32[768,128]{1,0:T(8,128)S(1)}, u32[]{:S(2)}, u32[]{:S(2)}) %collective-permute-start.27) | collective-permute-done | bytes 393248 | tf_op jit(solution)/shard_map/ppermute | solution.py:60
  151.2 2.3 collective-permute-start.29
  157.0 4.9 %collective-permute-start.95 = (f32[384,128]{1,0:T(8,128)S(1)}, f32[384,128]{1,0:T(8,128)S(1)}, u32[]{:S(2)}, u32[]{:S(2)}) collective-permute-start(f32[384,128]{1,0:T(8,128)S(1)} %get-tuple-element.47), channel_id=1, source_target_pairs={{0,1},{1,0},{2,3},{3,2},{4,5},{5,4},{6,7},{7,6},{8,9},{9,8},{10,11... | collective-permute-start | bytes 589832 | tf_op jit(solution)/shard_map/ppermute | solution.py:60
  164.4 1.8 collective-permute-start.32
  167.5 2.2 collective-permute-start.98
  169.7 4.7 %collective-permute-start.33 = (f32[96,128]{1,0:T(8,128)S(1)}, f32[96,128]{1,0:T(8,128)S(1)}, u32[]{:S(2)}, u32[]{:S(2)}) collective-permute-start(f32[96,128]{1,0:T(8,128)S(1)} %get-tuple-element.59), channel_id=1, source_target_pairs={{0,32},{1,33},{2,34},{3,35},{4,36},{5,37},{6,38},{7,39},{8,40},{9,... | collective-permute-start | bytes 147464 | tf_op jit(solution)/shard_map/ppermute | solution.py:60
  174.4 4.7 %collective-permute-start.99 = (f32[96,128]{1,0:T(8,128)S(1)}, f32[96,128]{1,0:T(8,128)S(1)}, u32[]{:S(2)}, u32[]{:S(2)}) collective-permute-start(f32[96,128]{1,0:T(8,128)S(1)} %get-tuple-element.69), channel_id=1, source_target_pairs={{0,32},{1,33},{2,34},{3,35},{4,36},{5,37},{6,38},{7,39},{8,40},{9,... | collective-permute-start | bytes 147464 | tf_op jit(solution)/shard_map/ppermute | solution.py:60
  180.3 3.1 collective-permute-start.35
  191.3 2.1 collective-permute-start.105
  193.4 6.8 %collective-permute-done.38.refs_1_ = f32[768,128]{1,0:T(8,128)S(1)} collective-permute-done((f32[768,128]{1,0:T(8,128)S(1)}, f32[768,128]{1,0:T(8,128)S(1)}, u32[]{:S(2)}, u32[]{:S(2)}) %collective-permute-start.38) | collective-permute-done | bytes 393248 | tf_op jit(solution)/shard_map/ppermute | solution.py:60
  209.8 3.8 %collective-permute-start.106 = (f32[384,128]{1,0:T(8,128)S(1)}, f32[384,128]{1,0:T(8,128)S(1)}, u32[]{:S(2)}, u32[]{:S(2)}) collective-permute-start(f32[384,128]{1,0:T(8,128)S(1)} %get-tuple-element.49), channel_id=1, source_target_pairs={{0,1},{1,0},{2,3},{3,2},{4,5},{5,4},{6,7},{7,6},{8,9},{9,8},{10,11... | collective-permute-start | bytes 589832 | tf_op jit(solution)/shard_map/ppermute | solution.py:60
  213.6 1.9 collective-permute-start.41
  216.0 2.0 collective-permute-start.43
  219.4 2.0 collective-permute-start.109
  221.4 4.5 %collective-permute-start.44 = (f32[96,128]{1,0:T(8,128)S(1)}, f32[96,128]{1,0:T(8,128)S(1)}, u32[]{:S(2)}, u32[]{:S(2)}) collective-permute-start(f32[96,128]{1,0:T(8,128)S(1)} %get-tuple-element.57), channel_id=1, source_target_pairs={{0,32},{1,33},{2,34},{3,35},{4,36},{5,37},{6,38},{7,39},{8,40},{9,... | collective-permute-start | bytes 147464 | tf_op jit(solution)/shard_map/ppermute | solution.py:60
  225.9 3.7 %collective-permute-start.110 = (f32[96,128]{1,0:T(8,128)S(1)}, f32[96,128]{1,0:T(8,128)S(1)}, u32[]{:S(2)}, u32[]{:S(2)}) collective-permute-start(f32[96,128]{1,0:T(8,128)S(1)} %get-tuple-element.67), channel_id=1, source_target_pairs={{0,32},{1,33},{2,34},{3,35},{4,36},{5,37},{6,38},{7,39},{8,40},{9,... | collective-permute-start | bytes 147464 | tf_op jit(solution)/shard_map/ppermute | solution.py:60
  230.9 3.1 collective-permute-start.46
  235.6 2.1 collective-permute-start.112
  242.3 2.4 collective-permute-start.116
  244.7 6.8 %collective-permute-done.49.refs_1_ = f32[768,128]{1,0:T(8,128)S(1)} collective-permute-done((f32[768,128]{1,0:T(8,128)S(1)}, f32[768,128]{1,0:T(8,128)S(1)}, u32[]{:S(2)}, u32[]{:S(2)}) %collective-permute-start.49) | collective-permute-done | bytes 393248 | tf_op jit(solution)/shard_map/ppermute | solution.py:60
  255.0 2.5 collective-permute-start.51
  261.0 4.7 %collective-permute-start.117 = (f32[384,128]{1,0:T(8,128)S(1)}, f32[384,128]{1,0:T(8,128)S(1)}, u32[]{:S(2)}, u32[]{:S(2)}) collective-permute-start(f32[384,128]{1,0:T(8,128)S(1)} %get-tuple-element.51), channel_id=1, source_target_pairs={{0,1},{1,0},{2,3},{3,2},{4,5},{5,4},{6,7},{7,6},{8,9},{9,8},{10,11... | collective-permute-start | bytes 589832 | tf_op jit(solution)/shard_map/ppermute | solution.py:60
  265.7 1.8 collective-permute-start.52
  273.4 3.2 collective-permute-start.55
  277.6 3.2 collective-permute-start.121
  282.1 2.6 collective-permute-start.57
  286.3 3.2 collective-permute-start.123
  290.0 2.6 collective-permute-start.61
  293.7 2.7 collective-permute-start.127
  296.3 6.6 %collective-permute-done.60.refs_1_ = f32[768,128]{1,0:T(8,128)S(1)} collective-permute-done((f32[768,128]{1,0:T(8,128)S(1)}, f32[768,128]{1,0:T(8,128)S(1)}, u32[]{:S(2)}, u32[]{:S(2)}) %collective-permute-start.60) | collective-permute-done | bytes 393248 | tf_op jit(solution)/shard_map/ppermute | solution.py:60
  306.4 2.5 collective-permute-start.62
  308.9 3.7 copy-done.1
  322.8 2.1 collective-permute-start.131
  326.0 3.2 collective-permute-done.130
  331.4 12.4 %all_to_all.15 = f32[16,8,256]{2,1,0:T(8,128)S(1)} all-to-all(f32[16,8,256]{2,1,0:T(8,128)S(1)} %fusion), channel_id=1, replica_groups=mesh['x'=4,'zh'=2,'y'=4,'zl'=4,'core'=2] {'x','y'}, dimensions={0} | all-to-all | bytes 262144 | tf_op jit(solution)/shard_map/all_to_all | solution.py:206
  343.8 11.3 %all_to_all.16 = f32[8,8,256]{2,1,0:T(8,128)S(1)} all-to-all(f32[8,8,256]{2,1,0:T(8,128)S(1)} %broadcast_in_dim.6), channel_id=1, replica_groups=mesh['x'=4,'zh'=2,'y'=4,'zl'=4,'core'=2] {'zh','zl'}, dimensions={0} | all-to-all | bytes 131072 | tf_op jit(solution)/shard_map/all_to_all | solution.py:207
  355.1 10.2 %all_to_all.17 = f32[16,8,256]{2,1,0:T(8,128)S(1)} all-to-all(f32[16,8,256]{2,1,0:T(8,128)S(1)} %broadcast_in_dim.7), channel_id=1, replica_groups=mesh['x'=4,'zh'=2,'y'=4,'zl'=4,'core'=2] {'x','y'}, dimensions={0} | all-to-all | bytes 262144 | tf_op jit(solution)/shard_map/all_to_all | solution.py:208
  365.3 4.3 %collective-permute-start.133 = (f32[128,256]{1,0:T(8,128)S(1)}, f32[128,256]{1,0:T(8,128)S(1)}, u32[]{:S(2)}, u32[]{:S(2)}) collective-permute-start(f32[128,256]{1,0:T(8,128)S(1)} %bitcast.16), channel_id=1, source_target_pairs={{0,1},{1,0},{2,3},{3,2},{4,5},{5,4},{6,7},{7,6},{8,9},{9,8},{10,11... | collective-permute-start | bytes 393224 | tf_op jit(solution)/shard_map/ppermute | solution.py:60
  (362 shorter events, 121.8 us)
Async XLA Ops:
  1.5 9.3 %collective-permute-start = (f32[96,128]{1,0:T(8,128)S(1)}, f32[96,128]{1,0:T(8,128)S(1)}, u32[]{:S(2)}, u32[]{:S(2)}) collective-permute-start(f32[96,128]{1,0:T(8,128)S(1)} %get-tuple-element.28), channel_id=1, source_target_pairs={{0,32},{1,33},{2,34},{3,35},{4,36},{5,37},{6,38},{7,39},{8,40},{9,... | collective-permute-start | bytes 147464 | tf_op jit(solution)/shard_map/ppermute | solution.py:60
  18.3 10.4 %collective-permute-start.5 = (f32[768,128]{1,0:T(8,128)S(1)}, f32[768,128]{1,0:T(8,128)S(1)}, u32[]{:S(2)}, u32[]{:S(2)}) collective-permute-start(f32[768,128]{1,0:T(8,128)S(1)} %constant_dynamic-update-slice_fusion.2.refs_1_), channel_id=1, source_target_pairs={{0,64},{1,9},{2,66},{3,11},{4,68},{5,13},{6,70},{7,15},{8,72},{9,1... | collective-permute-start | bytes 1179656 | tf_op jit(solution)/shard_map/ppermute | solution.py:60
  22.7 17.2 %collective-permute-start.6 = (f32[768,128]{1,0:T(8,128)S(1)}, f32[768,128]{1,0:T(8,128)S(1)}, u32[]{:S(2)}, u32[]{:S(2)}) collective-permute-start(f32[768,128]{1,0:T(8,128)S(1)} %constant_dynamic-update-slice_fusion.2.refs_1_), channel_id=1, source_target_pairs={{0,192},{1,25},{2,194},{3,27},{4,196},{5,29},{6,198},{7,31},{8,200... | collective-permute-start | bytes 1179656 | tf_op jit(solution)/shard_map/ppermute | solution.py:60
  24.3 17.2 %collective-permute-start.4 = (f32[768,128]{1,0:T(8,128)S(1)}, f32[768,128]{1,0:T(8,128)S(1)}, u32[]{:S(2)}, u32[]{:S(2)}) collective-permute-start(f32[768,128]{1,0:T(8,128)S(1)} %constant_dynamic-update-slice_fusion.2.refs_1_), channel_id=1, source_target_pairs={{0,128},{1,17},{2,130},{3,19},{4,132},{5,21},{6,134},{7,23},{8,136... | collective-permute-start | bytes 1179656 | tf_op jit(solution)/shard_map/ppermute | solution.py:60
  25.9 24.1 %collective-permute-start.71 = (f32[768,128]{1,0:T(8,128)S(1)}, f32[768,128]{1,0:T(8,128)S(1)}, u32[]{:S(2)}, u32[]{:S(2)}) collective-permute-start(f32[768,128]{1,0:T(8,128)S(1)} %constant_dynamic-update-slice_fusion.34.refs_1_), channel_id=1, source_target_pairs={{0,64},{1,9},{2,66},{3,11},{4,68},{5,13},{6,70},{7,15},{8,72},{9,1... | collective-permute-start | bytes 1179656 | tf_op jit(solution)/shard_map/ppermute | solution.py:60
  27.0 22.9 %collective-permute-start.72 = (f32[768,128]{1,0:T(8,128)S(1)}, f32[768,128]{1,0:T(8,128)S(1)}, u32[]{:S(2)}, u32[]{:S(2)}) collective-permute-start(f32[768,128]{1,0:T(8,128)S(1)} %constant_dynamic-update-slice_fusion.34.refs_1_), channel_id=1, source_target_pairs={{0,192},{1,25},{2,194},{3,27},{4,196},{5,29},{6,198},{7,31},{8,200... | collective-permute-start | bytes 1179656 | tf_op jit(solution)/shard_map/ppermute | solution.py:60
  28.6 22.9 %collective-permute-start.70 = (f32[768,128]{1,0:T(8,128)S(1)}, f32[768,128]{1,0:T(8,128)S(1)}, u32[]{:S(2)}, u32[]{:S(2)}) collective-permute-start(f32[768,128]{1,0:T(8,128)S(1)} %constant_dynamic-update-slice_fusion.34.refs_1_), channel_id=1, source_target_pairs={{0,128},{1,17},{2,130},{3,19},{4,132},{5,21},{6,134},{7,23},{8,136... | collective-permute-start | bytes 1179656 | tf_op jit(solution)/shard_map/ppermute | solution.py:60
  42.5 10.2 %collective-permute-start.7 = (f32[384,128]{1,0:T(8,128)S(1)}, f32[384,128]{1,0:T(8,128)S(1)}, u32[]{:S(2)}, u32[]{:S(2)}) collective-permute-start(f32[384,128]{1,0:T(8,128)S(1)} %get-tuple-element.30), channel_id=1, source_target_pairs={{0,1},{1,0},{2,3},{3,2},{4,5},{5,4},{6,7},{7,6},{8,9},{9,8},{10,11... | collective-permute-start | bytes 589832 | tf_op jit(solution)/shard_map/ppermute | solution.py:60
  56.6 10.5 %collective-permute-start.74 = (f32[96,128]{1,0:T(8,128)S(1)}, f32[96,128]{1,0:T(8,128)S(1)}, u32[]{:S(2)}, u32[]{:S(2)}) collective-permute-start(f32[96,128]{1,0:T(8,128)S(1)} %get-tuple-element.109), channel_id=1, source_target_pairs={{0,2},{1,3},{2,4},{3,5},{4,6},{5,7},{6,0},{7,1},{8,10},{9,11},{10,... | collective-permute-start | bytes 147464 | tf_op jit(solution)/shard_map/ppermute | solution.py:60
  61.8 8.8 %collective-permute-start.11 = (f32[96,128]{1,0:T(8,128)S(1)}, f32[96,128]{1,0:T(8,128)S(1)}, u32[]{:S(2)}, u32[]{:S(2)}) collective-permute-start(f32[96,128]{1,0:T(8,128)S(1)} %get-tuple-element.62), channel_id=1, source_target_pairs={{0,32},{1,33},{2,34},{3,35},{4,36},{5,37},{6,38},{7,39},{8,40},{9,... | collective-permute-start | bytes 147464 | tf_op jit(solution)/shard_map/ppermute | solution.py:60
  75.0 8.2 %collective-permute-start.79 = (f32[192,128]{1,0:T(8,128)S(1)}, f32[192,128]{1,0:T(8,128)S(1)}, u32[]{:S(2)}, u32[]{:S(2)}) collective-permute-start(f32[192,128]{1,0:T(8,128)S(1)} %pad_maximum_fusion.6), channel_id=1, source_target_pairs={{0,16},{1,129},{2,18},{3,131},{4,20},{5,133},{6,22},{7,135},{8,24}... | collective-permute-start | bytes 294920 | tf_op jit(solution)/shard_map/ppermute | solution.py:60
  78.2 10.9 %collective-permute-start.16 = (f32[768,128]{1,0:T(8,128)S(1)}, f32[768,128]{1,0:T(8,128)S(1)}, u32[]{:S(2)}, u32[]{:S(2)}) collective-permute-start(f32[768,128]{1,0:T(8,128)S(1)} %constant_dynamic-update-slice_fusion.7.refs_1_), channel_id=1, source_target_pairs={{0,64},{1,9},{2,66},{3,11},{4,68},{5,13},{6,70},{7,15},{8,72},{9,1... | collective-permute-start | bytes 1179656 | tf_op jit(solution)/shard_map/ppermute | solution.py:60
  80.9 10.9 %collective-permute-start.17 = (f32[768,128]{1,0:T(8,128)S(1)}, f32[768,128]{1,0:T(8,128)S(1)}, u32[]{:S(2)}, u32[]{:S(2)}) collective-permute-start(f32[768,128]{1,0:T(8,128)S(1)} %constant_dynamic-update-slice_fusion.7.refs_1_), channel_id=1, source_target_pairs={{0,192},{1,25},{2,194},{3,27},{4,196},{5,29},{6,198},{7,31},{8,200... | collective-permute-start | bytes 1179656 | tf_op jit(solution)/shard_map/ppermute | solution.py:60
  82.0 12.9 %collective-permute-start.15 = (f32[768,128]{1,0:T(8,128)S(1)}, f32[768,128]{1,0:T(8,128)S(1)}, u32[]{:S(2)}, u32[]{:S(2)}) collective-permute-start(f32[768,128]{1,0:T(8,128)S(1)} %constant_dynamic-update-slice_fusion.7.refs_1_), channel_id=1, source_target_pairs={{0,128},{1,17},{2,130},{3,19},{4,132},{5,21},{6,134},{7,23},{8,136... | collective-permute-start | bytes 1179656 | tf_op jit(solution)/shard_map/ppermute | solution.py:60
  83.2 20.4 %collective-permute-start.82 = (f32[768,128]{1,0:T(8,128)S(1)}, f32[768,128]{1,0:T(8,128)S(1)}, u32[]{:S(2)}, u32[]{:S(2)}) collective-permute-start(f32[768,128]{1,0:T(8,128)S(1)} %constant_dynamic-update-slice_fusion.39.refs_1_), channel_id=1, source_target_pairs={{0,64},{1,9},{2,66},{3,11},{4,68},{5,13},{6,70},{7,15},{8,72},{9,1... | collective-permute-start | bytes 1179656 | tf_op jit(solution)/shard_map/ppermute | solution.py:60
  85.7 18.0 %collective-permute-start.83 = (f32[768,128]{1,0:T(8,128)S(1)}, f32[768,128]{1,0:T(8,128)S(1)}, u32[]{:S(2)}, u32[]{:S(2)}) collective-permute-start(f32[768,128]{1,0:T(8,128)S(1)} %constant_dynamic-update-slice_fusion.39.refs_1_), channel_id=1, source_target_pairs={{0,192},{1,25},{2,194},{3,27},{4,196},{5,29},{6,198},{7,31},{8,200... | collective-permute-start | bytes 1179656 | tf_op jit(solution)/shard_map/ppermute | solution.py:60
  89.1 16.1 %collective-permute-start.81 = (f32[768,128]{1,0:T(8,128)S(1)}, f32[768,128]{1,0:T(8,128)S(1)}, u32[]{:S(2)}, u32[]{:S(2)}) collective-permute-start(f32[768,128]{1,0:T(8,128)S(1)} %constant_dynamic-update-slice_fusion.39.refs_1_), channel_id=1, source_target_pairs={{0,128},{1,17},{2,130},{3,19},{4,132},{5,21},{6,134},{7,23},{8,136... | collective-permute-start | bytes 1179656 | tf_op jit(solution)/shard_map/ppermute | solution.py:60
  95.9 13.8 %collective-permute-start.18 = (f32[384,128]{1,0:T(8,128)S(1)}, f32[384,128]{1,0:T(8,128)S(1)}, u32[]{:S(2)}, u32[]{:S(2)}) collective-permute-start(f32[384,128]{1,0:T(8,128)S(1)} %get-tuple-element.32), channel_id=1, source_target_pairs={{0,1},{1,0},{2,3},{3,2},{4,5},{5,4},{6,7},{7,6},{8,9},{9,8},{10,11... | collective-permute-start | bytes 589832 | tf_op jit(solution)/shard_map/ppermute | solution.py:60
  113.2 8.6 %collective-permute-start.85 = (f32[96,128]{1,0:T(8,128)S(1)}, f32[96,128]{1,0:T(8,128)S(1)}, u32[]{:S(2)}, u32[]{:S(2)}) collective-permute-start(f32[96,128]{1,0:T(8,128)S(1)} %get-tuple-element.106), channel_id=1, source_target_pairs={{0,2},{1,3},{2,4},{3,5},{4,6},{5,7},{6,0},{7,1},{8,10},{9,11},{10,... | collective-permute-start | bytes 147464 | tf_op jit(solution)/shard_map/ppermute | solution.py:60
  113.5 8.2 %collective-permute-start.86 = (f32[96,128]{1,0:T(8,128)S(1)}, f32[96,128]{1,0:T(8,128)S(1)}, u32[]{:S(2)}, u32[]{:S(2)}) collective-permute-start(f32[96,128]{1,0:T(8,128)S(1)} %get-tuple-element.108), channel_id=1, source_target_pairs={{0,4},{1,5},{2,6},{3,7},{4,0},{5,1},{6,2},{7,3},{8,12},{9,13},{10,... | collective-permute-start | bytes 147464 | tf_op jit(solution)/shard_map/ppermute | solution.py:60
  117.1 8.8 %collective-permute-start.22 = (f32[96,128]{1,0:T(8,128)S(1)}, f32[96,128]{1,0:T(8,128)S(1)}, u32[]{:S(2)}, u32[]{:S(2)}) collective-permute-start(f32[96,128]{1,0:T(8,128)S(1)} %get-tuple-element.61), channel_id=1, source_target_pairs={{0,32},{1,33},{2,34},{3,35},{4,36},{5,37},{6,38},{7,39},{8,40},{9,... | collective-permute-start | bytes 147464 | tf_op jit(solution)/shard_map/ppermute | solution.py:60
  121.8 8.8 %collective-permute-start.88 = (f32[96,128]{1,0:T(8,128)S(1)}, f32[96,128]{1,0:T(8,128)S(1)}, u32[]{:S(2)}, u32[]{:S(2)}) collective-permute-start(f32[96,128]{1,0:T(8,128)S(1)} %get-tuple-element.71), channel_id=1, source_target_pairs={{0,32},{1,33},{2,34},{3,35},{4,36},{5,37},{6,38},{7,39},{8,40},{9,... | collective-permute-start | bytes 147464 | tf_op jit(solution)/shard_map/ppermute | solution.py:60
  126.0 8.0 %collective-permute-start.23 = (f32[192,128]{1,0:T(8,128)S(1)}, f32[192,128]{1,0:T(8,128)S(1)}, u32[]{:S(2)}, u32[]{:S(2)}) collective-permute-start(f32[192,128]{1,0:T(8,128)S(1)} %pad_maximum_fusion.2), channel_id=1, source_target_pairs={{0,8},{1,65},{2,10},{3,67},{4,12},{5,69},{6,14},{7,71},{8,16},{9,7... | collective-permute-start | bytes 294920 | tf_op jit(solution)/shard_map/ppermute | solution.py:60
  126.0 9.1 %collective-permute-start.24 = (f32[192,128]{1,0:T(8,128)S(1)}, f32[192,128]{1,0:T(8,128)S(1)}, u32[]{:S(2)}, u32[]{:S(2)}) collective-permute-start(f32[192,128]{1,0:T(8,128)S(1)} %pad_maximum_fusion.2), channel_id=1, source_target_pairs={{0,16},{1,129},{2,18},{3,131},{4,20},{5,133},{6,22},{7,135},{8,24}... | collective-permute-start | bytes 294920 | tf_op jit(solution)/shard_map/ppermute | solution.py:60
  135.2 12.4 %collective-permute-start.27 = (f32[768,128]{1,0:T(8,128)S(1)}, f32[768,128]{1,0:T(8,128)S(1)}, u32[]{:S(2)}, u32[]{:S(2)}) collective-permute-start(f32[768,128]{1,0:T(8,128)S(1)} %constant_dynamic-update-slice_fusion.12.refs_1_), channel_id=1, source_target_pairs={{0,64},{1,9},{2,66},{3,11},{4,68},{5,13},{6,70},{7,15},{8,72},{9,1... | collective-permute-start | bytes 1179656 | tf_op jit(solution)/shard_map/ppermute | solution.py:60
  135.3 13.2 %collective-permute-start.28 = (f32[768,128]{1,0:T(8,128)S(1)}, f32[768,128]{1,0:T(8,128)S(1)}, u32[]{:S(2)}, u32[]{:S(2)}) collective-permute-start(f32[768,128]{1,0:T(8,128)S(1)} %constant_dynamic-update-slice_fusion.12.refs_1_), channel_id=1, source_target_pairs={{0,192},{1,25},{2,194},{3,27},{4,196},{5,29},{6,198},{7,31},{8,200... | collective-permute-start | bytes 1179656 | tf_op jit(solution)/shard_map/ppermute | solution.py:60
  138.0 12.1 %collective-permute-start.26 = (f32[768,128]{1,0:T(8,128)S(1)}, f32[768,128]{1,0:T(8,128)S(1)}, u32[]{:S(2)}, u32[]{:S(2)}) collective-permute-start(f32[768,128]{1,0:T(8,128)S(1)} %constant_dynamic-update-slice_fusion.12.refs_1_), channel_id=1, source_target_pairs={{0,128},{1,17},{2,130},{3,19},{4,132},{5,21},{6,134},{7,23},{8,136... | collective-permute-start | bytes 1179656 | tf_op jit(solution)/shard_map/ppermute | solution.py:60
  138.2 16.1 %collective-permute-start.93 = (f32[768,128]{1,0:T(8,128)S(1)}, f32[768,128]{1,0:T(8,128)S(1)}, u32[]{:S(2)}, u32[]{:S(2)}) collective-permute-start(f32[768,128]{1,0:T(8,128)S(1)} %constant_dynamic-update-slice_fusion.44.refs_1_), channel_id=1, source_target_pairs={{0,64},{1,9},{2,66},{3,11},{4,68},{5,13},{6,70},{7,15},{8,72},{9,1... | collective-permute-start | bytes 1179656 | tf_op jit(solution)/shard_map/ppermute | solution.py:60
  138.8 15.6 %collective-permute-start.94 = (f32[768,128]{1,0:T(8,128)S(1)}, f32[768,128]{1,0:T(8,128)S(1)}, u32[]{:S(2)}, u32[]{:S(2)}) collective-permute-start(f32[768,128]{1,0:T(8,128)S(1)} %constant_dynamic-update-slice_fusion.44.refs_1_), channel_id=1, source_target_pairs={{0,192},{1,25},{2,194},{3,27},{4,196},{5,29},{6,198},{7,31},{8,200... | collective-permute-start | bytes 1179656 | tf_op jit(solution)/shard_map/ppermute | solution.py:60
  147.7 8.3 %collective-permute-start.92 = (f32[768,128]{1,0:T(8,128)S(1)}, f32[768,128]{1,0:T(8,128)S(1)}, u32[]{:S(2)}, u32[]{:S(2)}) collective-permute-start(f32[768,128]{1,0:T(8,128)S(1)} %constant_dynamic-update-slice_fusion.44.refs_1_), channel_id=1, source_target_pairs={{0,128},{1,17},{2,130},{3,19},{4,132},{5,21},{6,134},{7,23},{8,136... | collective-permute-start | bytes 1179656 | tf_op jit(solution)/shard_map/ppermute | solution.py:60
  151.2 10.7 %collective-permute-start.29 = (f32[384,128]{1,0:T(8,128)S(1)}, f32[384,128]{1,0:T(8,128)S(1)}, u32[]{:S(2)}, u32[]{:S(2)}) collective-permute-start(f32[384,128]{1,0:T(8,128)S(1)} %get-tuple-element.34), channel_id=1, source_target_pairs={{0,1},{1,0},{2,3},{3,2},{4,5},{5,4},{6,7},{7,6},{8,9},{9,8},{10,11... | collective-permute-start | bytes 589832 | tf_op jit(solution)/shard_map/ppermute | solution.py:60
  157.0 9.3 %collective-permute-start.95 = (f32[384,128]{1,0:T(8,128)S(1)}, f32[384,128]{1,0:T(8,128)S(1)}, u32[]{:S(2)}, u32[]{:S(2)}) collective-permute-start(f32[384,128]{1,0:T(8,128)S(1)} %get-tuple-element.47), channel_id=1, source_target_pairs={{0,1},{1,0},{2,3},{3,2},{4,5},{5,4},{6,7},{7,6},{8,9},{9,8},{10,11... | collective-permute-start | bytes 589832 | tf_op jit(solution)/shard_map/ppermute | solution.py:60
  166.3 8.1 %collective-permute-start.96 = (f32[96,128]{1,0:T(8,128)S(1)}, f32[96,128]{1,0:T(8,128)S(1)}, u32[]{:S(2)}, u32[]{:S(2)}) collective-permute-start(f32[96,128]{1,0:T(8,128)S(1)} %get-tuple-element.103), channel_id=1, source_target_pairs={{0,2},{1,3},{2,4},{3,5},{4,6},{5,7},{6,0},{7,1},{8,10},{9,11},{10,... | collective-permute-start | bytes 147464 | tf_op jit(solution)/shard_map/ppermute | solution.py:60
  166.4 8.0 %collective-permute-start.97 = (f32[96,128]{1,0:T(8,128)S(1)}, f32[96,128]{1,0:T(8,128)S(1)}, u32[]{:S(2)}, u32[]{:S(2)}) collective-permute-start(f32[96,128]{1,0:T(8,128)S(1)} %get-tuple-element.105), channel_id=1, source_target_pairs={{0,4},{1,5},{2,6},{3,7},{4,0},{5,1},{6,2},{7,3},{8,12},{9,13},{10,... | collective-permute-start | bytes 147464 | tf_op jit(solution)/shard_map/ppermute | solution.py:60
  169.7 9.4 %collective-permute-start.33 = (f32[96,128]{1,0:T(8,128)S(1)}, f32[96,128]{1,0:T(8,128)S(1)}, u32[]{:S(2)}, u32[]{:S(2)}) collective-permute-start(f32[96,128]{1,0:T(8,128)S(1)} %get-tuple-element.59), channel_id=1, source_target_pairs={{0,32},{1,33},{2,34},{3,35},{4,36},{5,37},{6,38},{7,39},{8,40},{9,... | collective-permute-start | bytes 147464 | tf_op jit(solution)/shard_map/ppermute | solution.py:60
  174.4 9.1 %collective-permute-start.99 = (f32[96,128]{1,0:T(8,128)S(1)}, f32[96,128]{1,0:T(8,128)S(1)}, u32[]{:S(2)}, u32[]{:S(2)}) collective-permute-start(f32[96,128]{1,0:T(8,128)S(1)} %get-tuple-element.69), channel_id=1, source_target_pairs={{0,32},{1,33},{2,34},{3,35},{4,36},{5,37},{6,38},{7,39},{8,40},{9,... | collective-permute-start | bytes 147464 | tf_op jit(solution)/shard_map/ppermute | solution.py:60
  187.7 12.4 %collective-permute-start.38 = (f32[768,128]{1,0:T(8,128)S(1)}, f32[768,128]{1,0:T(8,128)S(1)}, u32[]{:S(2)}, u32[]{:S(2)}) collective-permute-start(f32[768,128]{1,0:T(8,128)S(1)} %constant_dynamic-update-slice_fusion.17.refs_1_), channel_id=1, source_target_pairs={{0,64},{1,9},{2,66},{3,11},{4,68},{5,13},{6,70},{7,15},{8,72},{9,1... | collective-permute-start | bytes 1179656 | tf_op jit(solution)/shard_map/ppermute | solution.py:60
  188.6 12.5 %collective-permute-start.39 = (f32[768,128]{1,0:T(8,128)S(1)}, f32[768,128]{1,0:T(8,128)S(1)}, u32[]{:S(2)}, u32[]{:S(2)}) collective-permute-start(f32[768,128]{1,0:T(8,128)S(1)} %constant_dynamic-update-slice_fusion.17.refs_1_), channel_id=1, source_target_pairs={{0,192},{1,25},{2,194},{3,27},{4,196},{5,29},{6,198},{7,31},{8,200... | collective-permute-start | bytes 1179656 | tf_op jit(solution)/shard_map/ppermute | solution.py:60
  190.5 12.3 %collective-permute-start.37 = (f32[768,128]{1,0:T(8,128)S(1)}, f32[768,128]{1,0:T(8,128)S(1)}, u32[]{:S(2)}, u32[]{:S(2)}) collective-permute-start(f32[768,128]{1,0:T(8,128)S(1)} %constant_dynamic-update-slice_fusion.17.refs_1_), channel_id=1, source_target_pairs={{0,128},{1,17},{2,130},{3,19},{4,132},{5,21},{6,134},{7,23},{8,136... | collective-permute-start | bytes 1179656 | tf_op jit(solution)/shard_map/ppermute | solution.py:60
  190.6 15.5 %collective-permute-start.104 = (f32[768,128]{1,0:T(8,128)S(1)}, f32[768,128]{1,0:T(8,128)S(1)}, u32[]{:S(2)}, u32[]{:S(2)}) collective-permute-start(f32[768,128]{1,0:T(8,128)S(1)} %constant_dynamic-update-slice_fusion.49.refs_1_), channel_id=1, source_target_pairs={{0,64},{1,9},{2,66},{3,11},{4,68},{5,13},{6,70},{7,15},{8,72},{9,1... | collective-permute-start | bytes 1179656 | tf_op jit(solution)/shard_map/ppermute | solution.py:60
  191.3 14.8 %collective-permute-start.105 = (f32[768,128]{1,0:T(8,128)S(1)}, f32[768,128]{1,0:T(8,128)S(1)}, u32[]{:S(2)}, u32[]{:S(2)}) collective-permute-start(f32[768,128]{1,0:T(8,128)S(1)} %constant_dynamic-update-slice_fusion.49.refs_1_), channel_id=1, source_target_pairs={{0,192},{1,25},{2,194},{3,27},{4,196},{5,29},{6,198},{7,31},{8,200... | collective-permute-start | bytes 1179656 | tf_op jit(solution)/shard_map/ppermute | solution.py:60
  200.1 8.6 %collective-permute-start.103 = (f32[768,128]{1,0:T(8,128)S(1)}, f32[768,128]{1,0:T(8,128)S(1)}, u32[]{:S(2)}, u32[]{:S(2)}) collective-permute-start(f32[768,128]{1,0:T(8,128)S(1)} %constant_dynamic-update-slice_fusion.49.refs_1_), channel_id=1, source_target_pairs={{0,128},{1,17},{2,130},{3,19},{4,132},{5,21},{6,134},{7,23},{8,136... | collective-permute-start | bytes 1179656 | tf_op jit(solution)/shard_map/ppermute | solution.py:60
  203.8 9.7 %collective-permute-start.40 = (f32[384,128]{1,0:T(8,128)S(1)}, f32[384,128]{1,0:T(8,128)S(1)}, u32[]{:S(2)}, u32[]{:S(2)}) collective-permute-start(f32[384,128]{1,0:T(8,128)S(1)} %get-tuple-element.36), channel_id=1, source_target_pairs={{0,1},{1,0},{2,3},{3,2},{4,5},{5,4},{6,7},{7,6},{8,9},{9,8},{10,11... | collective-permute-start | bytes 589832 | tf_op jit(solution)/shard_map/ppermute | solution.py:60
  209.8 8.2 %collective-permute-start.106 = (f32[384,128]{1,0:T(8,128)S(1)}, f32[384,128]{1,0:T(8,128)S(1)}, u32[]{:S(2)}, u32[]{:S(2)}) collective-permute-start(f32[384,128]{1,0:T(8,128)S(1)} %get-tuple-element.49), channel_id=1, source_target_pairs={{0,1},{1,0},{2,3},{3,2},{4,5},{5,4},{6,7},{7,6},{8,9},{9,8},{10,11... | collective-permute-start | bytes 589832 | tf_op jit(solution)/shard_map/ppermute | solution.py:60
  221.4 8.2 %collective-permute-start.44 = (f32[96,128]{1,0:T(8,128)S(1)}, f32[96,128]{1,0:T(8,128)S(1)}, u32[]{:S(2)}, u32[]{:S(2)}) collective-permute-start(f32[96,128]{1,0:T(8,128)S(1)} %get-tuple-element.57), channel_id=1, source_target_pairs={{0,32},{1,33},{2,34},{3,35},{4,36},{5,37},{6,38},{7,39},{8,40},{9,... | collective-permute-start | bytes 147464 | tf_op jit(solution)/shard_map/ppermute | solution.py:60
  225.9 8.1 %collective-permute-start.110 = (f32[96,128]{1,0:T(8,128)S(1)}, f32[96,128]{1,0:T(8,128)S(1)}, u32[]{:S(2)}, u32[]{:S(2)}) collective-permute-start(f32[96,128]{1,0:T(8,128)S(1)} %get-tuple-element.67), channel_id=1, source_target_pairs={{0,32},{1,33},{2,34},{3,35},{4,36},{5,37},{6,38},{7,39},{8,40},{9,... | collective-permute-start | bytes 147464 | tf_op jit(solution)/shard_map/ppermute | solution.py:60
  229.7 8.0 %collective-permute-start.45 = (f32[192,128]{1,0:T(8,128)S(1)}, f32[192,128]{1,0:T(8,128)S(1)}, u32[]{:S(2)}, u32[]{:S(2)}) collective-permute-start(f32[192,128]{1,0:T(8,128)S(1)} %pad_maximum_fusion.4), channel_id=1, source_target_pairs={{0,8},{1,65},{2,10},{3,67},{4,12},{5,69},{6,14},{7,71},{8,16},{9,7... | collective-permute-start | bytes 294920 | tf_op jit(solution)/shard_map/ppermute | solution.py:60
  238.2 13.2 %collective-permute-start.49 = (f32[768,128]{1,0:T(8,128)S(1)}, f32[768,128]{1,0:T(8,128)S(1)}, u32[]{:S(2)}, u32[]{:S(2)}) collective-permute-start(f32[768,128]{1,0:T(8,128)S(1)} %constant_dynamic-update-slice_fusion.22.refs_1_), channel_id=1, source_target_pairs={{0,64},{1,9},{2,66},{3,11},{4,68},{5,13},{6,70},{7,15},{8,72},{9,1... | collective-permute-start | bytes 1179656 | tf_op jit(solution)/shard_map/ppermute | solution.py:60
  240.0 12.4 %collective-permute-start.50 = (f32[768,128]{1,0:T(8,128)S(1)}, f32[768,128]{1,0:T(8,128)S(1)}, u32[]{:S(2)}, u32[]{:S(2)}) collective-permute-start(f32[768,128]{1,0:T(8,128)S(1)} %constant_dynamic-update-slice_fusion.22.refs_1_), channel_id=1, source_target_pairs={{0,192},{1,25},{2,194},{3,27},{4,196},{5,29},{6,198},{7,31},{8,200... | collective-permute-start | bytes 1179656 | tf_op jit(solution)/shard_map/ppermute | solution.py:60
  241.0 12.9 %collective-permute-start.48 = (f32[768,128]{1,0:T(8,128)S(1)}, f32[768,128]{1,0:T(8,128)S(1)}, u32[]{:S(2)}, u32[]{:S(2)}) collective-permute-start(f32[768,128]{1,0:T(8,128)S(1)} %constant_dynamic-update-slice_fusion.22.refs_1_), channel_id=1, source_target_pairs={{0,128},{1,17},{2,130},{3,19},{4,132},{5,21},{6,134},{7,23},{8,136... | collective-permute-start | bytes 1179656 | tf_op jit(solution)/shard_map/ppermute | solution.py:60
  241.9 16.3 %collective-permute-start.115 = (f32[768,128]{1,0:T(8,128)S(1)}, f32[768,128]{1,0:T(8,128)S(1)}, u32[]{:S(2)}, u32[]{:S(2)}) collective-permute-start(f32[768,128]{1,0:T(8,128)S(1)} %constant_dynamic-update-slice_fusion.54.refs_1_), channel_id=1, source_target_pairs={{0,64},{1,9},{2,66},{3,11},{4,68},{5,13},{6,70},{7,15},{8,72},{9,1... | collective-permute-start | bytes 1179656 | tf_op jit(solution)/shard_map/ppermute | solution.py:60
  242.3 16.0 %collective-permute-start.116 = (f32[768,128]{1,0:T(8,128)S(1)}, f32[768,128]{1,0:T(8,128)S(1)}, u32[]{:S(2)}, u32[]{:S(2)}) collective-permute-start(f32[768,128]{1,0:T(8,128)S(1)} %constant_dynamic-update-slice_fusion.54.refs_1_), channel_id=1, source_target_pairs={{0,192},{1,25},{2,194},{3,27},{4,196},{5,29},{6,198},{7,31},{8,200... | collective-permute-start | bytes 1179656 | tf_op jit(solution)/shard_map/ppermute | solution.py:60
  251.5 8.4 %collective-permute-start.114 = (f32[768,128]{1,0:T(8,128)S(1)}, f32[768,128]{1,0:T(8,128)S(1)}, u32[]{:S(2)}, u32[]{:S(2)}) collective-permute-start(f32[768,128]{1,0:T(8,128)S(1)} %constant_dynamic-update-slice_fusion.54.refs_1_), channel_id=1, source_target_pairs={{0,128},{1,17},{2,130},{3,19},{4,132},{5,21},{6,134},{7,23},{8,136... | collective-permute-start | bytes 1179656 | tf_op jit(solution)/shard_map/ppermute | solution.py:60
  255.0 10.7 %collective-permute-start.51 = (f32[384,128]{1,0:T(8,128)S(1)}, f32[384,128]{1,0:T(8,128)S(1)}, u32[]{:S(2)}, u32[]{:S(2)}) collective-permute-start(f32[384,128]{1,0:T(8,128)S(1)} %get-tuple-element.38), channel_id=1, source_target_pairs={{0,1},{1,0},{2,3},{3,2},{4,5},{5,4},{6,7},{7,6},{8,9},{9,8},{10,11... | collective-permute-start | bytes 589832 | tf_op jit(solution)/shard_map/ppermute | solution.py:60
  261.0 8.7 %collective-permute-start.117 = (f32[384,128]{1,0:T(8,128)S(1)}, f32[384,128]{1,0:T(8,128)S(1)}, u32[]{:S(2)}, u32[]{:S(2)}) collective-permute-start(f32[384,128]{1,0:T(8,128)S(1)} %get-tuple-element.51), channel_id=1, source_target_pairs={{0,1},{1,0},{2,3},{3,2},{4,5},{5,4},{6,7},{7,6},{8,9},{9,8},{10,11... | collective-permute-start | bytes 589832 | tf_op jit(solution)/shard_map/ppermute | solution.py:60
  280.8 8.7 %collective-permute-start.56 = (f32[192,128]{1,0:T(8,128)S(1)}, f32[192,128]{1,0:T(8,128)S(1)}, u32[]{:S(2)}, u32[]{:S(2)}) collective-permute-start(f32[192,128]{1,0:T(8,128)S(1)} %pad_maximum_fusion.5), channel_id=1, source_target_pairs={{0,8},{1,65},{2,10},{3,67},{4,12},{5,69},{6,14},{7,71},{8,16},{9,7... | collective-permute-start | bytes 294920 | tf_op jit(solution)/shard_map/ppermute | solution.py:60
  289.9 13.0 %collective-permute-start.60 = (f32[768,128]{1,0:T(8,128)S(1)}, f32[768,128]{1,0:T(8,128)S(1)}, u32[]{:S(2)}, u32[]{:S(2)}) collective-permute-start(f32[768,128]{1,0:T(8,128)S(1)} %constant_dynamic-update-slice_fusion.27.refs_1_), channel_id=1, source_target_pairs={{0,64},{1,9},{2,66},{3,11},{4,68},{5,13},{6,70},{7,15},{8,72},{9,1... | collective-permute-start | bytes 1179656 | tf_op jit(solution)/shard_map/ppermute | solution.py:60
  290.0 13.8 %collective-permute-start.61 = (f32[768,128]{1,0:T(8,128)S(1)}, f32[768,128]{1,0:T(8,128)S(1)}, u32[]{:S(2)}, u32[]{:S(2)}) collective-permute-start(f32[768,128]{1,0:T(8,128)S(1)} %constant_dynamic-update-slice_fusion.27.refs_1_), channel_id=1, source_target_pairs={{0,192},{1,25},{2,194},{3,27},{4,196},{5,29},{6,198},{7,31},{8,200... | collective-permute-start | bytes 1179656 | tf_op jit(solution)/shard_map/ppermute | solution.py:60
  292.6 12.7 %collective-permute-start.59 = (f32[768,128]{1,0:T(8,128)S(1)}, f32[768,128]{1,0:T(8,128)S(1)}, u32[]{:S(2)}, u32[]{:S(2)}) collective-permute-start(f32[768,128]{1,0:T(8,128)S(1)} %constant_dynamic-update-slice_fusion.27.refs_1_), channel_id=1, source_target_pairs={{0,128},{1,17},{2,130},{3,19},{4,132},{5,21},{6,134},{7,23},{8,136... | collective-permute-start | bytes 1179656 | tf_op jit(solution)/shard_map/ppermute | solution.py:60
  293.6 19.9 %collective-permute-start.126 = (f32[768,128]{1,0:T(8,128)S(1)}, f32[768,128]{1,0:T(8,128)S(1)}, u32[]{:S(2)}, u32[]{:S(2)}) collective-permute-start(f32[768,128]{1,0:T(8,128)S(1)} %constant_dynamic-update-slice_fusion.59.refs_1_), channel_id=1, source_target_pairs={{0,64},{1,9},{2,66},{3,11},{4,68},{5,13},{6,70},{7,15},{8,72},{9,1... | collective-permute-start | bytes 1179656 | tf_op jit(solution)/shard_map/ppermute | solution.py:60
  293.7 19.8 %collective-permute-start.127 = (f32[768,128]{1,0:T(8,128)S(1)}, f32[768,128]{1,0:T(8,128)S(1)}, u32[]{:S(2)}, u32[]{:S(2)}) collective-permute-start(f32[768,128]{1,0:T(8,128)S(1)} %constant_dynamic-update-slice_fusion.59.refs_1_), channel_id=1, source_target_pairs={{0,192},{1,25},{2,194},{3,27},{4,196},{5,29},{6,198},{7,31},{8,200... | collective-permute-start | bytes 1179656 | tf_op jit(solution)/shard_map/ppermute | solution.py:60
  302.9 12.1 %collective-permute-start.125 = (f32[768,128]{1,0:T(8,128)S(1)}, f32[768,128]{1,0:T(8,128)S(1)}, u32[]{:S(2)}, u32[]{:S(2)}) collective-permute-start(f32[768,128]{1,0:T(8,128)S(1)} %constant_dynamic-update-slice_fusion.59.refs_1_), channel_id=1, source_target_pairs={{0,128},{1,17},{2,130},{3,19},{4,132},{5,21},{6,134},{7,23},{8,136... | collective-permute-start | bytes 1179656 | tf_op jit(solution)/shard_map/ppermute | solution.py:60
  306.4 10.9 %collective-permute-start.62 = (f32[384,128]{1,0:T(8,128)S(1)}, f32[384,128]{1,0:T(8,128)S(1)}, u32[]{:S(2)}, u32[]{:S(2)}) collective-permute-start(f32[384,128]{1,0:T(8,128)S(1)} %get-tuple-element.40), channel_id=1, source_target_pairs={{0,1},{1,0},{2,3},{3,2},{4,5},{5,4},{6,7},{7,6},{8,9},{9,8},{10,11... | collective-permute-start | bytes 589832 | tf_op jit(solution)/shard_map/ppermute | solution.py:60
  321.3 7.9 %collective-permute-start.130 = (f32[96,128]{1,0:T(8,128)S(1)}, f32[96,128]{1,0:T(8,128)S(1)}, u32[]{:S(2)}, u32[]{:S(2)}) collective-permute-start(f32[96,128]{1,0:T(8,128)S(1)} %get-tuple-element.95), channel_id=1, source_target_pairs={{0,4},{1,5},{2,6},{3,7},{4,0},{5,1},{6,2},{7,3},{8,12},{9,13},{10,... | collective-permute-start | bytes 147464 | tf_op jit(solution)/shard_map/ppermute | solution.py:60
  (74 other events, 741.9 us)
